TPU v7x, 32 devices: a whole 2x2x4 slice. The times are simulated.
32 devices in a mesh: groups: 2 (over y), qry: 4 (over x, core), ref: 4 (over z).
Axes of the slice: x: 2, y: 2, z: 4, core: 2. Of those that a mesh axis runs over, the one named last changes fastest.
Arguments:
- query_feats: bfloat16 [1024, 9, 3840], P(('groups', 'qry')), parts along dimension 0, may hold values from -6 to 6
- ref_feats: bfloat16 [256, 4, 9, 3840], P(('groups', 'ref'), 'qry'), parts along dimension 0, may hold values from -6 to 6
- pair_table: int32 [8, 4], P('groups'), parts along dimension 0, may hold values from 0 to 1, as said below
- lengths: int32 [4], P('groups'), parts along dimension 0, may hold values from 1 to 96, 128 in all
- query_len: int32 [2], P('groups'), parts along dimension 0, may hold values from 64 to 128
- conv1_weight: float32 [3, 3, 32], replicated, may hold values from -2 to 2
- conv1_bias: float32 [32], replicated, may hold values from -3 to 3
- conv2_weight: bfloat16 [3, 3, 64, 32], replicated, may hold values from -0.375 to 0.375
- conv2_bias: float32 [64], replicated, may hold values from -3 to 3
- conv3_weight: bfloat16 [3, 3, 128, 64], replicated, may hold values from -0.25 to 0.25
- conv3_bias: float32 [128], replicated, may hold values from -3 to 3
- conv4_weight: bfloat16 [128], replicated, may hold values from -0.5 to 0.5
- conv4_bias: float32 [1], replicated, may hold values from -3 to 3
Outputs:
- score_map: float32 [256, 128], P(('groups', 'qry'), 'ref'), parts along dimension 0
- video_scores: float32 [4], P('groups'), parts along dimension 0
There are 2 independent parts, one for each index of `groups`. A program takes and returns all parts, laid end to end along the dimension named above; an argument that names none is the same for every part. Nothing has to cross between parts.
Inputs may be any that keep to these rules, and one draw needn't show every extreme that they name: `pair_table`: in each row, at most 1 of the 1 tiles in the block of one index of ref are 1, and some such block holds exactly 1 in every draw.
All inputs are finite; a program needn't handle non-finite values.
Results may differ from a plain program's by a relative error of at most 0.01.
Values may be sent and summed in bfloat16 or wider, within the bound.
A program may use at most 128 MiB of HBM per device.

v0:
```python
import functools
import math

import jax
import jax.numpy as jnp
import numpy as np
from jax import lax
from jax.experimental import pallas as pl
from jax.experimental.pallas import tpu as pltpu
from jax.sharding import PartitionSpec as P

MESH = pl.DeviceIdType.MESH
HALO = 8
PITCH = 40
LEAD = 48


def whole_kernel(
    chips, others, regions, frames, scale, chunk, pair_ref, lengths_ref, len_ref, b4_ref,
    w1_ref, b1_ref, w2_ref, b2_ref, w3_ref, b3_ref, w4_ref, q_hbm, r_hbm,
    scores_ref, totals_ref,
    q_buf, r_buf, acc, sims_buf, map_buf, z_buf, x_buf, first_buf, second_buf, w2_full, w3_full,
    peaks_buf, sums_buf,
    q_sem, own_sem, send_x, recv_x, send_s, recv_s, send_h, recv_h, send_p, recv_p, send_t, recv_t,
):
    depth = r_hbm.shape[1]
    steps = depth // chunk
    shard = r_hbm.shape[0] // regions
    parts = regions * frames // 384
    me = lax.axis_index("qry")
    chip = me // 2
    core = me % 2
    sibling = chip * 2 + (1 - core)
    right = ((chip + 1) % chips) * 2 + core
    senders = 2 * chips
    col = lax.axis_index("ref")

    def reachable(move_q, move_r):
        fits = (me + move_q >= 0) & (me + move_q < senders)
        return fits & (col + move_r >= 0) & (col + move_r < others)

    def cols(c):
        return pl.ds(pl.multiple_of(c * chunk, 128), chunk)

    def own_copy(c):
        return pltpu.make_async_copy(
            r_hbm.at[:, cols(c)], r_buf.at[0, :, cols(c)], own_sem.at[c]
        )

    def q_copy(c):
        return pltpu.make_async_copy(q_hbm.at[:, cols(c)], q_buf.at[:, cols(c)], q_sem.at[c])

    def to_right(step, c):
        source = r_hbm if step == 0 else r_buf.at[2 * step]
        return pltpu.make_async_remote_copy(
            src_ref=source.at[:, cols(c)],
            dst_ref=r_buf.at[2 * step + 2, :, cols(c)],
            send_sem=send_x.at[step, c],
            recv_sem=recv_x.at[step, c],
            device_id={"qry": right},
            device_id_type=MESH,
        )

    def to_sibling(step, c):
        source = r_hbm if step == 0 else r_buf.at[2 * step]
        return pltpu.make_async_remote_copy(
            src_ref=source.at[:, cols(c)],
            dst_ref=r_buf.at[2 * step + 1, :, cols(c)],
            send_sem=send_s.at[step, c],
            recv_sem=recv_s.at[step, c],
            device_id={"qry": sibling},
            device_id_type=MESH,
        )

    def start_own(c, carry):
        own_copy(c).start()
        q_copy(c).start()
        return carry

    lax.fori_loop(0, steps, start_own, 0)
    map_buf[...] = jnp.zeros_like(map_buf)
    barrier = pltpu.get_barrier_semaphore()
    for k in range(1, senders):
        device = {"qry": (me + k) % senders}
        pl.semaphore_signal(barrier, inc=1, device_id=device, device_id_type=MESH)
    for k in range(1, others):
        device = {"ref": (col + k) % others}
        pl.semaphore_signal(barrier, inc=1, device_id=device, device_id_type=MESH)
    for move_q in (1, senders - 1):
        for move_r in (1, others - 1):
            device = {"qry": (me + move_q) % senders, "ref": (col + move_r) % others}
            pl.semaphore_signal(barrier, inc=1, device_id=device, device_id_type=MESH)
    pl.semaphore_wait(barrier, senders - 1 + others - 1 + 4)

    def start_sends(c, carry):
        to_right(0, c).start()
        to_sibling(0, c).start()
        return carry

    lax.fori_loop(0, steps, start_sends, 0)

    def multiply(slot, side, c):
        block = r_buf[slot, :, cols(c)]

        def one_part(i, carry):
            rows = pl.ds(pl.multiple_of(i * 384, 128), 384)
            term = lax.dot_general(
                block, q_buf[rows, cols(c)], (((1,), (1,)), ((), ())),
                preferred_element_type=jnp.float32,
            )
            kept = acc[side, i]
            acc[side, i] = jnp.where(c == 0, term, kept + term)
            return carry

        lax.fori_loop(0, parts, one_part, 0)

    def finish(step, side):
        origin = (chip + chips - step) % chips
        source = origin * 2 + (core if side == 0 else 1 - core)
        total = jnp.zeros((shard, frames), jnp.float32)
        for i in range(parts):
            best = jnp.max(acc[side, i].reshape(regions, shard, 384), axis=0)
            for k in range(384 // frames):
                total = total + best[:, k * frames : (k + 1) * frames]
        sims_buf[source] = total * (scale * active)

    active = pair_ref[me, col].astype(jnp.float32)
    acc[...] = jnp.zeros_like(acc)
    build_weights(w2_ref, w3_ref, w2_full, w3_full)

    def first_own(c, carry):
        own_copy(c).wait()
        q_copy(c).wait()
        multiply(0, 0, c)
        return carry

    lax.fori_loop(0, steps, first_own, 0)
    finish(0, 0)

    def first_sibling(c, carry):
        to_sibling(0, c).wait_recv()
        multiply(1, 1, c)
        return carry

    lax.fori_loop(0, steps, first_sibling, 0)
    finish(0, 1)
    for step in range(1, chips):

        def later(c, carry):
            to_right(step - 1, c).wait_recv()
            to_sibling(step, c).start()
            if step < chips - 1:
                to_right(step, c).start()
            multiply(2 * step, 0, c)
            to_sibling(step, c).wait_recv()
            multiply(2 * step + 1, 1, c)
            return carry

        lax.fori_loop(0, steps, later, 0)
        finish(step, 0)
        finish(step, 1)

    def drain(c, carry):
        for step in range(chips):
            to_sibling(step, c).wait_send()
            if step < chips - 1:
                to_right(step, c).wait_send()
        return carry

    lax.fori_loop(0, steps, drain, 0)

    for b in range(senders):
        map_buf.at[1][pl.ds(HALO + b, shard, stride=senders), :] = sims_buf[b]

    def halo_copy(k, move_q, move_r):
        if move_r == 0:
            source, target = pl.ds(HALO, frames), pl.ds(HALO, frames)
        elif move_r == 1:
            source, target = pl.ds(frames, HALO), pl.ds(0, HALO)
        else:
            source, target = pl.ds(HALO, HALO), pl.ds(HALO + frames, HALO)
        return pltpu.make_async_remote_copy(
            src_ref=map_buf.at[1, source],
            dst_ref=map_buf.at[1 - move_q, target],
            send_sem=send_h.at[k],
            recv_sem=recv_h.at[k],
            device_id={"qry": me + move_q, "ref": col + move_r},
            device_id_type=MESH,
        )

    moves = [(q, r) for q in (-1, 1, 0) for r in (-1, 1, 0) if (q, r) != (0, 0)]
    for k, (move_q, move_r) in enumerate(moves):

        @pl.when(reachable(move_q, move_r))
        def _():
            halo_copy(k, move_q, move_r).start()

    for k, (move_q, move_r) in enumerate(moves):

        @pl.when(reachable(-move_q, -move_r))
        def _():
            halo_copy(k, move_q, move_r).wait_recv()

    for k, (move_q, move_r) in enumerate(moves):

        @pl.when(reachable(move_q, move_r))
        def _():
            halo_copy(k, move_q, move_r).wait_send()

    tiles = frames // 4
    scores = network(
        tiles, (me * tiles, col * tiles, senders * tiles, others * tiles), map_buf, w1_ref, b1_ref,
        b2_ref, b3_ref, w4_ref, z_buf, x_buf, first_buf, second_buf, w2_full, w3_full,
    ) + b4_ref[0]
    scores_ref[...] = scores
    slot_f = lax.broadcasted_iota(jnp.int32, scores.shape, 0)
    column = slot_f + (col * tiles - 2)
    own = (slot_f >= 2) & (slot_f < 2 + tiles)
    peaks_buf[0] = jnp.zeros_like(peaks_buf[0])
    begin = jnp.int32(0)
    for v in range(lengths_ref.shape[0]):
        end = begin + lengths_ref[v]
        member = own & (column >= begin) & (column < end)
        peaks_buf[0, v : v + 1, :PITCH] = jnp.max(
            jnp.where(member, scores, -jnp.inf), axis=0, keepdims=True
        )
        begin = end

    def peak_copy(k):
        return pltpu.make_async_remote_copy(
            src_ref=peaks_buf.at[0],
            dst_ref=peaks_buf.at[k],
            send_sem=send_p.at[k],
            recv_sem=recv_p.at[k],
            device_id={"ref": (col + k) % others},
            device_id_type=MESH,
        )

    def sum_copy(k):
        return pltpu.make_async_remote_copy(
            src_ref=sums_buf.at[0],
            dst_ref=sums_buf.at[k],
            send_sem=send_t.at[k],
            recv_sem=recv_t.at[k],
            device_id={"qry": (me + k) % senders},
            device_id_type=MESH,
        )

    for k in range(1, others):
        peak_copy(k).start()
    for k in range(1, others):
        peak_copy(k).wait_recv()
    peaks = jnp.max(peaks_buf[...], axis=0)
    lane = lax.broadcasted_iota(jnp.int32, peaks.shape, 1)
    counted = (lane >= 2) & (lane < 2 + tiles) & (lane + (me * tiles - 2) < len_ref[0])
    partial_sum = jnp.sum(jnp.where(counted, peaks, 0.0), axis=1, keepdims=True)
    sums_buf[0] = jnp.broadcast_to(partial_sum, peaks.shape)
    for k in range(1, senders):
        sum_copy(k).start()
    for k in range(1, senders):
        sum_copy(k).wait_recv()
    totals_ref[...] = jnp.sum(sums_buf[...], axis=0) / len_ref[0].astype(jnp.float32)
    for k in range(1, others):
        peak_copy(k).wait_send()
    for k in range(1, senders):
        sum_copy(k).wait_send()


def build_weights(w2_ref, w3_ref, w2_full, w3_full):
    w2_full[...] = jnp.zeros_like(w2_full)
    taps = {(0, 0): 0, (0, 1): 1, (1, 0): 2, (1, 1): -1}
    for g in range(2):
        for h in range(2):
            for a in range(2):
                for b in range(2):
                    row = ((g * 2 + h) * 4 + a * 2 + b) * 32
                    for u in range(2):
                        for v in range(2):
                            di = taps[g, a] - u + 1
                            dj = taps[h, b] - v + 1
                            if 0 <= di < 3 and 0 <= dj < 3:
                                col = u * 128 + v * 64
                                w2_full[row : row + 32, col : col + 64] = w2_ref[di * 3 + dj]
    for k in range(9):
        w3_full[k * 64 : (k + 1) * 64, :] = w3_ref[k]
    w3_full[576:640, :] = jnp.zeros((64, 128), jnp.bfloat16)


def network(
    tiles, where_ref, map_ref, w1_ref, b1_ref, b2_ref, b3_ref, w4_ref,
    z_buf, x_buf, first_buf, second_buf, w2_full, w3_full,
):
    side = tiles + 4
    rows = side * PITCH
    wide = map_ref.shape[1]
    frames = map_ref.shape[2]
    lane = lax.broadcasted_iota(jnp.int32, (1, 128), 1)
    low_a = lane < 64
    low_b = (lane % 64) < 32

    source = lax.broadcasted_iota(jnp.int32, (3 * frames, 128), 0)
    target = lax.broadcasted_iota(jnp.int32, (3 * frames, 128), 1)
    whole = jnp.concatenate([map_ref[0], map_ref[1], map_ref[2]], axis=1)
    high = whole.astype(jnp.bfloat16)
    lower = (whole - high.astype(jnp.float32)).astype(jnp.bfloat16)
    z_buf[...] = jnp.zeros_like(z_buf)
    for rr in range(6):
        pick = jnp.where(source == 4 * target + (frames - 9) + rr, 1.0, 0.0).astype(jnp.bfloat16)
        for part, value in enumerate((high, lower)):
            z_buf[part, 8 : 8 + wide, rr * 128 : (rr + 1) * 128] = jnp.dot(
                value, pick, preferred_element_type=jnp.float32
            )
    for block in range(side):
        pieces = []
        for part in (0, 1, 0):
            for rr in range(6):
                pieces.append(
                    z_buf[part, 4 * block + 7 : 4 * block + 15, rr * 128 : (rr + 1) * 128]
                )
        flat = jnp.concatenate(pieces, axis=0)
        x_buf[block * PITCH : (block + 1) * PITCH, :] = jnp.transpose(flat)[:PITCH]

    shape = (side, PITCH, 128)
    at_f = lax.broadcasted_iota(jnp.int32, shape, 0) + (where_ref[1] - 2)
    at_p = lax.broadcasted_iota(jnp.int32, shape, 1) + (where_ref[0] - 2)
    inside = (at_f >= 0) & (at_f < where_ref[3]) & (at_p >= 0) & (at_p < where_ref[2])
    inside = jnp.where(inside, 1.0, 0.0).reshape(rows, 128)

    made = jnp.dot(
        x_buf[...].astype(jnp.bfloat16), w1_ref[...], preferred_element_type=jnp.float32
    )
    best = jnp.maximum(
        jnp.maximum(made[:, 0:128], made[:, 128:256]),
        jnp.maximum(made[:, 256:384], made[:, 384:512]),
    )
    first = jnp.maximum(best + b1_ref[...], 0.0)
    first = jnp.where(inside > 0.5, first, 0.0).astype(jnp.bfloat16).astype(jnp.float32)
    first_buf[0:LEAD, :] = jnp.zeros((LEAD, 128), jnp.float32)
    first_buf[LEAD + rows :, :] = jnp.zeros((LEAD, 128), jnp.float32)
    first_buf[LEAD : LEAD + rows, :] = first

    start = LEAD - PITCH
    more = rows + 2 * PITCH
    shifted = jnp.where(
        low_a, first_buf[start + 1 : start + 1 + more, :], first_buf[start - 1 : start - 1 + more, :]
    )
    across = jnp.where(
        low_b, first_buf[LEAD + PITCH : LEAD + PITCH + rows, :], first_buf[start : start + rows, :]
    )
    both = jnp.where(low_b, shifted[2 * PITCH :], shifted[:rows])
    stacked = jnp.concatenate(
        [first, across, shifted[PITCH : PITCH + rows], both], axis=1
    ).astype(jnp.bfloat16)
    made = jnp.dot(stacked, w2_full[...], preferred_element_type=jnp.float32)
    best = jnp.maximum(made[:, 0:128], made[:, 128:256])
    best = jnp.maximum(best, pltpu.roll(best, 64, 1))
    second = jnp.maximum(best + b2_ref[...], 0.0)
    second = jnp.where(inside > 0.5, second, 0.0).astype(jnp.bfloat16).astype(jnp.float32)
    second_buf[0:LEAD, :] = jnp.zeros((LEAD, 128), jnp.float32)
    second_buf[LEAD + rows :, :] = jnp.zeros((LEAD, 128), jnp.float32)
    second_buf[LEAD : LEAD + rows, :] = second

    def moved(k):
        di, dj = k // 3, k % 3
        begin = LEAD + (dj - 1) * PITCH + di - 1
        return second_buf[begin : begin + rows, :]

    groups = []
    for k in range(0, 9, 2):
        groups.append(jnp.where(low_a, moved(k), moved(k + 1)) if k < 8 else moved(k))
    stacked = jnp.concatenate(groups, axis=1).astype(jnp.bfloat16)
    made = jnp.dot(stacked, w3_full[...], preferred_element_type=jnp.float32)
    third = jnp.maximum(made + b3_ref[...], 0.0).astype(jnp.bfloat16).astype(jnp.float32)
    weighted = third * w4_ref[...]
    return jnp.sum(weighted.reshape(side, PITCH, 128), axis=2)


def first_matrix(weight):
    outputs = weight.shape[2]
    table = np.zeros((6, 8, 2, 2, 2, 2, 9), np.float32)
    for a in range(2):
        for b in range(2):
            for u in range(2):
                for v in range(2):
                    for di in range(3):
                        for dj in range(3):
                            table[2 * a + u + di, 2 * b + v + dj, u, v, a, b, di * 3 + dj] = 1.0
    full = jnp.dot(
        table.reshape(48 * 16, 9), weight.reshape(9, outputs), precision=lax.Precision.HIGHEST
    ).reshape(48, 16 * outputs)
    high = lax.reduce_precision(full, 8, 7)
    return jnp.concatenate([high, high, full - high], axis=0).astype(jnp.bfloat16)


def body(
    query_feats, ref_feats, pair_table, lengths, query_len, conv1_weight, conv1_bias,
    conv2_weight, conv2_bias, conv3_weight, conv3_bias, conv4_weight, conv4_bias,
):
    senders = lax.axis_size("qry")
    others = lax.axis_size("ref")
    frames, regions, depth = query_feats.shape
    query_mat = jnp.transpose(query_feats, (1, 0, 2)).reshape(regions * frames, depth)
    ref_mat = jnp.transpose(ref_feats, (1, 2, 0, 3)).reshape(-1, depth)
    videos = lengths.shape[0]
    video_rows = -(-videos // 8) * 8
    shard_rows = ref_mat.shape[0]
    chips = senders // 2
    chunk = 256 if depth % 256 == 0 else depth
    steps = depth // chunk
    parts = regions * frames // 384
    tiles = frames // 4
    side = tiles + 4
    rows = side * PITCH
    scale = 1.0 / (regions * math.sqrt(depth))
    vmem = pl.BlockSpec(memory_space=pltpu.VMEM)
    smem = pl.BlockSpec(memory_space=pltpu.SMEM)
    hbm = pl.BlockSpec(memory_space=pl.ANY)
    dma = pltpu.SemaphoreType.DMA
    scores, totals = pl.pallas_call(
        functools.partial(whole_kernel, chips, others, regions, frames, scale, chunk),
        out_shape=(
            jax.ShapeDtypeStruct((side, PITCH), jnp.float32),
            jax.ShapeDtypeStruct((video_rows, 128), jnp.float32),
        ),
        in_specs=[smem] * 4 + [vmem] * 7 + [hbm] * 2,
        out_specs=(vmem, vmem),
        scratch_shapes=[
            pltpu.VMEM(query_mat.shape, jnp.bfloat16),
            pltpu.VMEM((senders, shard_rows, depth), jnp.bfloat16),
            pltpu.VMEM((2, parts, shard_rows, 384), jnp.float32),
            pltpu.VMEM((senders, frames // senders, frames), jnp.float32),
            pltpu.VMEM((3, frames + 2 * HALO, frames), jnp.float32),
            pltpu.VMEM((2, frames + 4 * HALO, 768), jnp.float32),
            pltpu.VMEM((rows, 144), jnp.float32),
            pltpu.VMEM((rows + 2 * LEAD, 128), jnp.float32),
            pltpu.VMEM((rows + 2 * LEAD, 128), jnp.float32),
            pltpu.VMEM((512, 256), jnp.bfloat16),
            pltpu.VMEM((640, 128), jnp.bfloat16),
            pltpu.VMEM((others, video_rows, 128), jnp.float32),
            pltpu.VMEM((senders, video_rows, 128), jnp.float32),
            dma((steps,)),
            dma((steps,)),
            dma((chips, steps)),
            dma((chips, steps)),
            dma((chips, steps)),
            dma((chips, steps)),
            dma((8,)),
            dma((8,)),
            dma((others,)),
            dma((others,)),
            dma((senders,)),
            dma((senders,)),
        ],
        compiler_params=pltpu.CompilerParams(
            collective_id=0, has_side_effects=True, vmem_limit_bytes=56 << 20
        ),
        name="whole",
    )(
        pair_table,
        lengths,
        query_len,
        conv4_bias,
        first_matrix(conv1_weight),
        jnp.tile(conv1_bias, 4)[None],
        jnp.transpose(conv2_weight, (0, 1, 3, 2)).reshape(
            9, conv2_weight.shape[3], conv2_weight.shape[2]
        ),
        jnp.tile(conv2_bias, 2)[None],
        jnp.transpose(conv3_weight, (0, 1, 3, 2)).reshape(
            9, conv3_weight.shape[3], conv3_weight.shape[2]
        ),
        conv3_bias[None],
        conv4_weight.astype(jnp.float32)[None],
        query_mat,
        ref_mat,
    )
    score_map = jnp.transpose(scores[2 : 2 + tiles, 2 : 2 + tiles])
    return (score_map, totals[:videos, 0])


def solution(mesh):
    placed = (
        P(("groups", "qry"), None, None),
        P(("groups", "ref"), "qry", None, None),
        P("groups", None),
        P("groups"),
        P("groups"),
    ) + (P(),) * 8
    return jax.shard_map(
        body,
        mesh=mesh,
        in_specs=placed,
        out_specs=(P(("groups", "qry"), "ref"), P("groups")),
        check_vma=False,
    )
```

profile of v0, /device:TPU:0, one launch (start us, length us, event | category | flops | bytes accessed | tf_op | source)
XLA Modules:
  0.0 85.8 jit_solution(11681865144311169362)
XLA Ops:
  0.6 0.7 reshape.24
  1.3 1.4 %fusion.1 = f32[768,32]{1,0:T(8,128)S(1)} fusion(f32[768,9]{1,0:T(8,128)} %constant.2.clone, f32[9,32]{1,0:T(8,128)S(1)} %reshape.24), kind=kOutput, calls=%fused_computation.7 | convolution fusion | flops 2654208 | bytes 127104 | tf_op jit(solution)/shard_map/dot_general | solution.py:388
  2.8 0.2 reshape.25
  3.0 0.7 pad_maximum_fusion.w1_ref
  3.7 0.7 tile.4
  4.3 0.6 broadcast_in_dim_tile.6.b1_ref
  4.9 0.7 tile.5
  5.6 0.6 broadcast_in_dim_tile.7.b2_ref
  6.2 1.2 %bitcast_convert_fusion.w4_ref = f32[1,128]{1,0:T(1,128)} fusion(bf16[128]{0:T(256)(128)(2,1)} %param.25), kind=kLoop, calls=%fused_computation.6 | loop fusion | flops 128 | bytes 768 | tf_op jit(solution)/shard_map/broadcast_in_dim | solution.py:473
  8.7 74.4 %whole.1 = (f32[36,40]{1,0:T(8,128)}, f32[8,128]{1,0:T(8,128)}) custom-call(s32[4,4]{1,0:T(4,128)} %pair_ref.1, s32[2]{0:T(128)} %lengths_ref.1, s32[1]{0:T(128)S(6)} %copy.21.len_ref, f32[1]{0:T(128)S(6)} %copy.22.b4_ref, bf16[144,512]{1,0:T(8,128)(2,1)} %pad_maximum_fusion.w1_ref, f32[1,128]{1,0:T(1,128)} %broadcast_in_dim_tile.6.b1_ref, ...), custom_call_target="tpu_custom_call" | custom-call | tf_op jit(solution)/shard_map/whole/pallas_call | solution.py:419
  83.0 0.8 slice_bitcast_fusion
  83.8 0.7 copy.19
  84.5 1.3 %slice_reduce_fusion = f32[2]{0:T(128)} fusion(f32[8,128]{1,0:T(8,128)} %get-tuple-element.5), kind=kLoop, calls=%fused_computation.5 | loop fusion | bytes 16 | tf_op jit(solution)/shard_map/slice | solution.py:478
  (1 shorter events, 0.0 us)
where the time goes:
time: 86.2 us; the launch traced here: 85.8 us
  Pallas kernels  74.4 us (86%)
  local copies, waits for them, and re-layouts  6.17 us (7%)
  between operations  1.95 us (2%)
  other arithmetic  1.91 us (2%)
  matrix products  1.45 us (2%)
    pallas_call x1, Pallas kernels, body(): pl.pallas_call(functools.partial(whole_kernel, chips, others, regions, fr...  74.4 us

commit v1 on v0

v1 whole, which is shorter than its diff:
```python
import functools
import math

import jax
import jax.numpy as jnp
from jax import lax
from jax.experimental import pallas as pl
from jax.experimental.pallas import tpu as pltpu
from jax.sharding import PartitionSpec as P

MESH = pl.DeviceIdType.MESH
HALO = 8
PITCH = 40
LEAD = 48
GROUP = 8
NT = (((1,), (1,)), ((), ()))


def spans(flags):
    found = []
    for k, flag in enumerate(flags):
        if flag and (k == 0 or not flags[k - 1]):
            found.append([k, k + 1])
        elif flag:
            found[-1][1] = k + 1
    return [tuple(span) for span in found]


def plan(chunks, frames, tiles, last):
    side = tiles + 4
    width = frames // chunks

    def early(frame):
        chunk = chunks - 1 if frame < 0 else 0 if frame >= frames else frame // width
        return chunk != last

    ready = []
    for j in range(side):
        ready.append(all(early(4 * (j - 2) + k) for k in range(-1, 5)))
    passes = [[ready], [[not flag for flag in ready]]]
    for layer in (1, 2):
        wanted = [layer <= j < side - layer for j in range(side)]
        before = passes[0][-1]
        now = [wanted[j] and all(before[j + k] for k in (-1, 0, 1)) for j in range(1, side - 1)]
        now = [False] + now + [False]
        passes[0].append(now)
        passes[1].append([wanted[j] and not now[j] for j in range(side)])
    return [[spans(flags) for flags in one] for one in passes]


def chunk_order(chunks, k):
    return k // 2 + (k % 2) * (chunks - 1 - 2 * (k // 2))


def whole_kernel(
    chips, others, scale, cuts,
    pair_hbm, lengths_hbm, len_hbm, b4_hbm, w1_hbm, b1_hbm, w2_hbm, b2_hbm, w3_hbm, b3_hbm,
    w4_hbm, q_hbm, r_hbm,
    scores_ref, totals_ref,
    pair_ref, lengths_ref, len_ref, b4_ref, w1_ref, b1_ref, w2_ref, b2_ref, w3_ref, b3_ref, w4_ref,
    q_buf, r_own, r_far, acc, sims_buf, map_buf, z_buf, x_buf, first_buf, second_buf,
    w1_rep, w1_flat, w1_full, w2_full, w3_full, b1_full, b2_full, score_buf, peaks_buf,
    small_sem, q_sem, own_sem, send_o, recv_o, send_x, recv_x, send_s, recv_s, send_h, recv_h,
    send_p, recv_p,
):
    regions, shard, depth = r_hbm.shape
    frames = q_hbm.shape[0] // regions
    chunks = shard // GROUP
    width = GROUP * 2 * chips
    tiles = frames // 4
    last = chunk_order(chunks, chunks - 1)
    me = lax.axis_index("qry")
    chip = me // 2
    core = me % 2
    sibling = chip * 2 + (1 - core)
    right = ((chip + 1) % chips) * 2 + core
    senders = 2 * chips
    col = lax.axis_index("ref")
    peers = senders * others
    mine = me * others + col

    smalls = [
        pltpu.make_async_copy(source, target, small_sem.at[k])
        for k, (source, target) in enumerate(
            (
                (w1_hbm, w1_ref), (b1_hbm, b1_ref), (w2_hbm, w2_ref), (b2_hbm, b2_ref),
                (w3_hbm, w3_ref), (b3_hbm, b3_ref), (w4_hbm, w4_ref), (pair_hbm, pair_ref),
                (lengths_hbm, lengths_ref), (len_hbm, len_ref), (b4_hbm, b4_ref),
            )
        )
    ]

    def piece(p):
        return pl.ds(cuts[p], cuts[p + 1] - cuts[p])

    pieces = len(cuts) - 1

    def rows_of(g):
        return pl.ds(pl.multiple_of(g * GROUP, GROUP), GROUP)

    def own_copy(g):
        return pltpu.make_async_copy(r_hbm.at[:, rows_of(g)], r_own.at[0, g], own_sem.at[g])

    def own_to_sibling(g):
        return pltpu.make_async_remote_copy(
            src_ref=r_hbm.at[:, rows_of(g)],
            dst_ref=r_own.at[1, g],
            send_sem=send_o.at[g],
            recv_sem=recv_o.at[g],
            device_id={"qry": sibling},
            device_id_type=MESH,
        )

    def q_copy(k):
        rows = pl.ds(k * frames, frames)
        return pltpu.make_async_copy(q_hbm.at[rows], q_buf.at[rows], q_sem.at[k])

    def to_right(step, g, p):
        if step == 0:
            source = r_hbm.at[:, rows_of(g), piece(p)]
        else:
            source = r_far.at[step - 1, g, 0, :, :, piece(p)]
        return pltpu.make_async_remote_copy(
            src_ref=source,
            dst_ref=r_far.at[step, g, 0, :, :, piece(p)],
            send_sem=send_x.at[step, g, p],
            recv_sem=recv_x.at[step, g, p],
            device_id={"qry": right},
            device_id_type=MESH,
        )

    def to_sibling(step, g, p):
        return pltpu.make_async_remote_copy(
            src_ref=r_far.at[step, g, 0, :, :, piece(p)],
            dst_ref=r_far.at[step, g, 1, :, :, piece(p)],
            send_sem=send_s.at[step, g, p],
            recv_sem=recv_s.at[step, g, p],
            device_id={"qry": sibling},
            device_id_type=MESH,
        )

    for k in range(regions):
        q_copy(k).start()
    for g in range(chunks):
        own_copy(g).start()
    map_buf[...] = jnp.zeros_like(map_buf)
    barrier = pltpu.get_barrier_semaphore()

    def greet(k, carry):
        peer = (mine + k) % peers
        device = {"qry": peer // others, "ref": peer % others}
        pl.semaphore_signal(barrier, inc=1, device_id=device, device_id_type=MESH)
        return carry

    lax.fori_loop(1, peers, greet, 0)
    for copy in smalls:
        copy.start()
    pl.semaphore_wait(barrier, peers - 1)

    def start_sends(k, carry):
        g = chunk_order(chunks, k)
        for p in range(pieces):
            to_right(0, g, p).start()
        return carry

    lax.fori_loop(0, chunks, start_sends, 0)
    for g in range(chunks):
        own_to_sibling(g).start()

    z_buf[...] = jnp.zeros_like(z_buf)
    first_buf[...] = jnp.zeros_like(first_buf)
    second_buf[...] = jnp.zeros_like(second_buf)
    peaks_buf[mine] = jnp.zeros(peaks_buf.shape[1:], jnp.float32)
    for copy in smalls:
        copy.wait()
    build_weights(
        w1_ref, w2_ref, w3_ref, b1_ref, b2_ref, w1_rep, w1_flat, w1_full, w2_full, w3_full,
        b1_full, b2_full,
    )
    factor = pair_ref[me, col].astype(jnp.float32) * scale

    def similar(product, blocks):
        best = jnp.max(product.reshape(blocks, regions, GROUP, regions * frames), axis=1)
        total = best[:, :, :frames]
        for k in range(1, regions):
            total = total + best[:, :, k * frames : (k + 1) * frames]
        return total * factor

    def near(side):
        product = lax.dot_general(
            r_own[side].reshape(chunks * regions * GROUP, depth), q_buf[...], NT,
            preferred_element_type=jnp.float32,
        )
        return similar(product, chunks).reshape(shard, frames)

    for k in range(regions):
        q_copy(k).wait()
    for g in range(chunks):
        own_copy(g).wait()

    def near_side(side, carry):
        @pl.when(side == 1)
        def _():
            for g in range(chunks):
                own_to_sibling(g).wait_recv()

        sims_buf[chip * 2 + side * (1 - core) + (1 - side) * core] = near(side)
        return carry

    lax.fori_loop(0, 2, near_side, 0)

    def sources(step):
        origin = (chip + chips - 1 - step) % chips
        return origin * 2 + core, origin * 2 + (1 - core)

    def arrive(step, g, p):
        to_right(step, g, p).wait_recv()
        to_sibling(step, g, p).start()
        if step < chips - 2:
            to_right(step + 1, g, p).start()

    def part(step, g, first_piece, final_piece):
        columns = pl.ds(cuts[first_piece], cuts[final_piece] - cuts[first_piece])
        block = r_far[step, g, :, :, :, columns].reshape(2 * regions * GROUP, columns.size)
        return lax.dot_general(
            block, q_buf[:, columns], NT, preferred_element_type=jnp.float32
        )

    def keep(step, g, product):
        total = similar(product, 2)
        for k, source in enumerate(sources(step)):
            sims_buf[source, rows_of(g)] = total[k]

    def middle(k, carry):
        g = chunk_order(chunks, k)
        for step in range(chips - 1):
            for p in range(pieces):
                arrive(step, g, p)
            for p in range(pieces):
                to_sibling(step, g, p).wait_recv()
            keep(step, g, part(step, g, 0, pieces))
        return carry

    lax.fori_loop(0, chunks - 1, middle, 0)

    def reachable(move_q, move_r):
        fits = (me + move_q >= 0) & (me + move_q < senders)
        return fits & (col + move_r >= 0) & (col + move_r < others)

    def halo_copy(k, move_q, move_r, g):
        if move_r == 0:
            source = target = pl.ds(HALO + g * width, width)
        elif move_r == 1:
            source, target = pl.ds(frames, HALO), pl.ds(0, HALO)
        else:
            source, target = pl.ds(HALO, HALO), pl.ds(HALO + frames, HALO)
        return pltpu.make_async_remote_copy(
            src_ref=map_buf.at[1, source],
            dst_ref=map_buf.at[1 - move_q, target],
            send_sem=send_h.at[k],
            recv_sem=recv_h.at[k],
            device_id={"qry": me + move_q, "ref": col + move_r},
            device_id_type=MESH,
        )

    moves = [(q, 0, g) for g in range(chunks) for q in (-1, 1)]
    moves += [(q, r, 0 if r < 0 else chunks - 1) for r in (-1, 1) for q in (-1, 1, 0)]
    moves = list(enumerate(moves))

    def spread(done):
        for g in done:
            for b in range(senders):
                rows = pl.ds(HALO + g * width + b, GROUP, stride=senders)
                map_buf.at[1][rows, :] = sims_buf[b, g * GROUP : (g + 1) * GROUP]
        now = [(k, q, r, g) for k, (q, r, g) in moves if g in done]
        for k, q, r, g in now:

            @pl.when(reachable(q, r))
            def _():
                halo_copy(k, q, r, g).start()

        for k, q, r, g in now:

            @pl.when(reachable(-q, -r))
            def _():
                halo_copy(k, q, r, g).wait_recv()

    where = (me * tiles, col * tiles, senders * tiles, others * tiles)
    before, after = plan(chunks, frames, tiles, last)

    def network(layers):
        for lo, hi in layers[0]:
            conv1(lo, hi, where, map_buf, w1_full, b1_full, z_buf, x_buf, first_buf)
        for lo, hi in layers[1]:
            conv2(lo, hi, where, w2_full, b2_full, first_buf, second_buf)
        for lo, hi in layers[2]:
            score_buf[lo:hi, :PITCH] = conv3(lo, hi, w3_full, b3_ref, w4_ref, second_buf)

    if chunks > 1:
        spread([g for g in range(chunks) if g != last])
        network(before)

    for step in range(chips - 1):
        for p in range(pieces):
            arrive(step, last, p)
            to_sibling(step, last, p).wait_recv()
            if p == 0:
                acc[...] = part(step, last, p, p + 1)
            elif p < pieces - 1:
                acc[...] += part(step, last, p, p + 1)
            else:
                keep(step, last, acc[...] + part(step, last, p, p + 1))
    spread([last])
    network(after)

    scores = score_buf[...] + b4_ref[0]
    slot_f = lax.broadcasted_iota(jnp.int32, scores.shape, 0)
    column = slot_f + (col * tiles - 2)
    own = (slot_f >= 2) & (slot_f < 2 + tiles)
    begin = jnp.int32(0)
    for v in range(lengths_ref.shape[0]):
        end = begin + lengths_ref[v]
        member = own & (column >= begin) & (column < end)
        peaks_buf[mine, v : v + 1, :] = jnp.max(
            jnp.where(member, scores, -jnp.inf), axis=0, keepdims=True
        )
        begin = end

    def peak_copy(k):
        peer = (mine + k) % peers
        return pltpu.make_async_remote_copy(
            src_ref=peaks_buf.at[mine],
            dst_ref=peaks_buf.at[mine],
            send_sem=send_p.at[k],
            recv_sem=recv_p.at[mine],
            device_id={"qry": peer // others, "ref": peer % others},
            device_id_type=MESH,
        )

    def peak_wait(k, carry):
        peer = (mine + k) % peers
        pltpu.make_async_remote_copy(
            src_ref=peaks_buf.at[peer],
            dst_ref=peaks_buf.at[peer],
            send_sem=send_p.at[k],
            recv_sem=recv_p.at[peer],
            device_id={"qry": peer // others, "ref": peer % others},
            device_id_type=MESH,
        ).wait_recv()
        return carry

    def peak_start(k, carry):
        peak_copy(k).start()
        return carry

    lax.fori_loop(1, peers, peak_start, 0)
    scores_ref[...] = jnp.transpose(scores)[2 : 2 + tiles, 2 : 2 + tiles]

    def drain(g, carry):
        own_to_sibling(g).wait_send()
        for step in range(chips - 1):
            for p in range(pieces):
                to_right(step, g, p).wait_send()
                to_sibling(step, g, p).wait_send()
        return carry

    lax.fori_loop(0, chunks, drain, 0)
    for k, (q, r, g) in moves:

        @pl.when(reachable(q, r))
        def _():
            halo_copy(k, q, r, g).wait_send()

    lax.fori_loop(1, peers, peak_wait, 0)
    lane = lax.broadcasted_iota(jnp.int32, peaks_buf.shape[1:], 1)
    total = jnp.zeros(peaks_buf.shape[1:], jnp.float32)
    for s in range(senders):
        best = jnp.max(peaks_buf[s * others : (s + 1) * others], axis=0)
        counted = (lane >= 2) & (lane < 2 + tiles) & (lane + (s * tiles - 2) < len_ref[0])
        total = total + jnp.where(counted, best, 0.0)
    total = jnp.sum(total, axis=1, keepdims=True) / len_ref[0].astype(jnp.float32)
    for v in range(lengths_ref.shape[0]):
        totals_ref[v] = jnp.sum(total[v : v + 1])

    def peak_drain(k, carry):
        peak_copy(k).wait_send()
        return carry

    lax.fori_loop(1, peers, peak_drain, 0)


def build_weights(
    w1_ref, w2_ref, w3_ref, b1_ref, b2_ref, w1_rep, w1_flat, w1_full, w2_full, w3_full,
    b1_full, b2_full,
):
    for k in range(4):
        lanes = slice(k * 32, (k + 1) * 32)
        b1_full[:, lanes] = b1_ref[...]
        for di in range(3):
            w1_rep[3 * di : 3 * di + 3, lanes] = w1_ref[di]
    for k in range(2):
        b2_full[:, k * 64 : (k + 1) * 64] = b2_ref[...]
    w1_flat[...] = jnp.zeros_like(w1_flat)
    for u in range(2):
        for v in range(2):
            for a in range(2):
                for b in range(2):
                    at = (a * 2 + b) * 32
                    col = (u * 2 + v) * 128 + at
                    for k in range(9):
                        row = (2 * a + u + k // 3) * 8 + 2 * b + v + k % 3
                        w1_flat[row : row + 1, col : col + 32] = w1_rep[k : k + 1, at : at + 32]
    flat = w1_flat[...]
    high = flat.astype(jnp.bfloat16)
    w1_full[0:48] = high
    w1_full[48:96] = high
    w1_full[96:144] = (flat - high.astype(jnp.float32)).astype(jnp.bfloat16)

    w2_full[...] = jnp.zeros_like(w2_full)
    taps = {(0, 0): 0, (0, 1): 1, (1, 0): 2, (1, 1): -1}
    for g in range(2):
        for h in range(2):
            for a in range(2):
                for b in range(2):
                    row = ((g * 2 + h) * 4 + a * 2 + b) * 32
                    for u in range(2):
                        for v in range(2):
                            di = taps[g, a] - u + 1
                            dj = taps[h, b] - v + 1
                            if 0 <= di < 3 and 0 <= dj < 3:
                                col = u * 128 + v * 64
                                w2_full[row : row + 32, col : col + 64] = w2_ref[di * 3 + dj]
    for k in range(9):
        w3_full[k * 64 : (k + 1) * 64, :] = w3_ref[k]
    w3_full[576:640, :] = jnp.zeros((64, 128), jnp.bfloat16)


def inside_map(lo, hi, where):
    shape = (hi - lo, PITCH, 128)
    at_f = lax.broadcasted_iota(jnp.int32, shape, 0) + (where[1] - 2 + lo)
    at_p = lax.broadcasted_iota(jnp.int32, shape, 1) + (where[0] - 2)
    inside = (at_f >= 0) & (at_f < where[3]) & (at_p >= 0) & (at_p < where[2])
    return jnp.where(inside, 1.0, 0.0).reshape((hi - lo) * PITCH, 128)


def conv1(lo, hi, where, map_ref, w1_full, b1_full, z_buf, x_buf, first_buf):
    wide, frames = map_ref.shape[1:]
    top = max(0, (4 * lo - 1) // 8 * 8)
    end = min(wide, -(-(4 * hi + 3) // 8) * 8)
    source = lax.broadcasted_iota(jnp.int32, (3 * frames, 128), 0)
    target = lax.broadcasted_iota(jnp.int32, (3 * frames, 128), 1)
    whole = jnp.concatenate([map_ref[k, top:end] for k in range(3)], axis=1)
    high = whole.astype(jnp.bfloat16)
    lower = (whole - high.astype(jnp.float32)).astype(jnp.bfloat16)
    for rr in range(6):
        pick = jnp.where(source == 4 * target + (frames - 9) + rr, 1.0, 0.0).astype(jnp.bfloat16)
        for part, value in enumerate((high, lower)):
            z_buf[part, 8 + top : 8 + end, rr * 128 : (rr + 1) * 128] = jnp.dot(
                value, pick, preferred_element_type=jnp.float32
            )
    for block in range(lo, hi):
        pieces = []
        for part in (0, 1, 0):
            for rr in range(6):
                pieces.append(
                    z_buf[part, 4 * block + 7 : 4 * block + 15, rr * 128 : (rr + 1) * 128]
                )
        flat = jnp.concatenate(pieces, axis=0)
        x_buf[block * PITCH : (block + 1) * PITCH, :] = jnp.transpose(flat)[:PITCH]

    made = jnp.dot(
        x_buf[lo * PITCH : hi * PITCH].astype(jnp.bfloat16), w1_full[...],
        preferred_element_type=jnp.float32,
    )
    best = jnp.maximum(
        jnp.maximum(made[:, 0:128], made[:, 128:256]),
        jnp.maximum(made[:, 256:384], made[:, 384:512]),
    )
    first = jnp.maximum(best + b1_full[...], 0.0)
    first = jnp.where(inside_map(lo, hi, where) > 0.5, first, 0.0)
    first = first.astype(jnp.bfloat16).astype(jnp.float32)
    first_buf[LEAD + lo * PITCH : LEAD + hi * PITCH, :] = first


def conv2(lo, hi, where, w2_full, b2_full, first_buf, second_buf):
    lane = lax.broadcasted_iota(jnp.int32, (1, 128), 1)
    low_a = lane < 64
    low_b = (lane % 64) < 32
    rows = (hi - lo) * PITCH
    here = LEAD + lo * PITCH
    start = here - PITCH
    more = rows + 2 * PITCH
    first = first_buf[here : here + rows, :]
    shifted = jnp.where(
        low_a, first_buf[start + 1 : start + 1 + more, :], first_buf[start - 1 : start - 1 + more, :]
    )
    across = jnp.where(
        low_b, first_buf[here + PITCH : here + PITCH + rows, :], first_buf[start : start + rows, :]
    )
    both = jnp.where(low_b, shifted[2 * PITCH :], shifted[:rows])
    stacked = jnp.concatenate(
        [first, across, shifted[PITCH : PITCH + rows], both], axis=1
    ).astype(jnp.bfloat16)
    made = jnp.dot(stacked, w2_full[...], preferred_element_type=jnp.float32)
    best = jnp.maximum(made[:, 0:128], made[:, 128:256])
    best = jnp.maximum(best, pltpu.roll(best, 64, 1))
    second = jnp.maximum(best + b2_full[...], 0.0)
    second = jnp.where(inside_map(lo, hi, where) > 0.5, second, 0.0)
    second_buf[here : here + rows, :] = second.astype(jnp.bfloat16).astype(jnp.float32)


def conv3(lo, hi, w3_full, b3_ref, w4_ref, second_buf):
    lane = lax.broadcasted_iota(jnp.int32, (1, 128), 1)
    low_a = lane < 64
    rows = (hi - lo) * PITCH

    def moved(k):
        di, dj = k // 3, k % 3
        begin = LEAD + (lo + dj - 1) * PITCH + di - 1
        return second_buf[begin : begin + rows, :]

    groups = []
    for k in range(0, 9, 2):
        groups.append(jnp.where(low_a, moved(k), moved(k + 1)) if k < 8 else moved(k))
    stacked = jnp.concatenate(groups, axis=1).astype(jnp.bfloat16)
    made = jnp.dot(stacked, w3_full[...], preferred_element_type=jnp.float32)
    third = jnp.maximum(made + b3_ref[...], 0.0).astype(jnp.bfloat16).astype(jnp.float32)
    weighted = third * w4_ref[...].astype(jnp.float32)
    return jnp.sum(weighted.reshape(hi - lo, PITCH, 128), axis=2)


def body(
    query_feats, ref_feats, pair_table, lengths, query_len, conv1_weight, conv1_bias,
    conv2_weight, conv2_bias, conv3_weight, conv3_bias, conv4_weight, conv4_bias,
):
    senders = lax.axis_size("qry")
    others = lax.axis_size("ref")
    frames, regions, depth = query_feats.shape
    query_mat = jnp.transpose(query_feats, (1, 0, 2)).reshape(regions * frames, depth)
    ref_mat = jnp.transpose(ref_feats, (1, 2, 0, 3)).reshape(regions, -1, depth)
    videos = lengths.shape[0]
    video_rows = -(-videos // 8) * 8
    shard = ref_mat.shape[1]
    chunks = shard // GROUP
    chips = senders // 2
    steps = max(1, chips - 1)
    cuts = [0, depth * 9 // 15 // 128 * 128, depth * 13 // 15 // 128 * 128, depth]
    pieces = len(cuts) - 1
    tiles = frames // 4
    side = tiles + 4
    rows = side * PITCH
    scale = 1.0 / (regions * math.sqrt(depth))
    vmem = pl.BlockSpec(memory_space=pltpu.VMEM)
    smem = pl.BlockSpec(memory_space=pltpu.SMEM)
    hbm = pl.BlockSpec(memory_space=pl.ANY)
    dma = pltpu.SemaphoreType.DMA
    f32, bf16 = jnp.float32, jnp.bfloat16
    operands = (
        pair_table,
        lengths,
        query_len,
        conv4_bias,
        conv1_weight,
        conv1_bias[None],
        jnp.transpose(conv2_weight, (0, 1, 3, 2)).reshape(
            9, conv2_weight.shape[3], conv2_weight.shape[2]
        ),
        conv2_bias[None],
        jnp.transpose(conv3_weight, (0, 1, 3, 2)).reshape(
            9, conv3_weight.shape[3], conv3_weight.shape[2]
        ),
        conv3_bias[None],
        conv4_weight[None],
        query_mat,
        ref_mat,
    )
    kept = [
        (pltpu.SMEM if k < 4 else pltpu.VMEM)(operand.shape, operand.dtype)
        for k, operand in enumerate(operands[:11])
    ]
    scores, totals = pl.pallas_call(
        functools.partial(whole_kernel, chips, others, scale, cuts),
        out_shape=(
            jax.ShapeDtypeStruct((tiles, tiles), f32),
            jax.ShapeDtypeStruct((videos,), f32),
        ),
        in_specs=[hbm] * len(operands),
        out_specs=(vmem, smem),
        scratch_shapes=kept + [
            pltpu.VMEM(query_mat.shape, bf16),
            pltpu.VMEM((2, chunks, regions, GROUP, depth), bf16),
            pltpu.VMEM((steps, chunks, 2, regions, GROUP, depth), bf16),
            pltpu.VMEM((2 * regions * GROUP, regions * frames), f32),
            pltpu.VMEM((senders, shard, frames), f32),
            pltpu.VMEM((3, frames + 2 * HALO, frames), f32),
            pltpu.VMEM((2, frames + 4 * HALO, 768), f32),
            pltpu.VMEM((rows, 144), f32),
            pltpu.VMEM((rows + 2 * LEAD, 128), f32),
            pltpu.VMEM((rows + 2 * LEAD, 128), f32),
            pltpu.VMEM((16, 128), f32),
            pltpu.VMEM((48, 512), f32),
            pltpu.VMEM((144, 512), bf16),
            pltpu.VMEM((512, 256), bf16),
            pltpu.VMEM((640, 128), bf16),
            pltpu.VMEM((1, 128), f32),
            pltpu.VMEM((1, 128), f32),
            pltpu.VMEM((-(-side // 8) * 8, 128), f32),
            pltpu.VMEM((senders * others, video_rows, 128), f32),
            dma((11,)),
            dma((regions,)),
            dma((chunks,)),
            dma((chunks,)),
            dma((chunks,)),
            dma((steps, chunks, pieces)),
            dma((steps, chunks, pieces)),
            dma((steps, chunks, pieces)),
            dma((steps, chunks, pieces)),
            dma((2 * chunks + 6,)),
            dma((2 * chunks + 6,)),
            dma((senders * others,)),
            dma((senders * others,)),
        ],
        compiler_params=pltpu.CompilerParams(
            collective_id=0, has_side_effects=True, vmem_limit_bytes=56 << 20
        ),
        name="whole",
    )(*operands)
    return (scores, totals)


def solution(mesh):
    placed = (
        P(("groups", "qry"), None, None),
        P(("groups", "ref"), "qry", None, None),
        P("groups", None),
        P("groups"),
        P("groups"),
    ) + (P(),) * 8
    return jax.shard_map(
        body,
        mesh=mesh,
        in_specs=placed,
        out_specs=(P(("groups", "qry"), "ref"), P("groups")),
        check_vma=False,
    )
```

time: 86.2 us -> 78.3 us (0.908)
  local copies, waits for them, and re-layouts: 6.17 us -> 2.46 us
  other arithmetic: 1.91 us -> 0 us
  matrix products: 1.45 us -> 0 us
    another operation x4 -> x0, local copies, waits for them, and re-layouts: 2.5 us -> none  [the longest x2 1.25 us: body(): jnp.tile(conv1_bias, 4)[None]]
    unnamed x1 -> x2, local copies, waits for them, and re-layouts: 0.68 us -> 2.46 us
    dot_general x1 -> x0, matrix products: 1.45 us -> none  [first_matrix(): jnp.dot(table.reshape(48 * 16, 9), weight.reshape(9, outputs), precision=...]
    slice x1 -> x0, local copies, waits for them, and re-layouts: 1.3 us -> none  [body(): return (score_map, totals[:videos, 0])]
    broadcast_in_dim x1 -> x0, other arithmetic: 1.23 us -> none  [body(): conv4_weight.astype(jnp.float32)[None]]
    reshape x2 -> x0, local copies, waits for them, and re-layouts: 0.88 us -> none  [the longest x1 0.7 us: first_matrix(): weight.reshape(9, outputs)]
where the time goes in v1:
time: 78.3 us; the launch traced here: 78 us
  Pallas kernels  73.6 us (94%)
  local copies, waits for them, and re-layouts  2.46 us (3%)
  between operations  1.93 us (2%)
    pallas_call x1, Pallas kernels, body(): pl.pallas_call(functools.partial(whole_kernel, chips, others, scale, cuts...  73.6 us
    unnamed x2, local copies, waits for them, and re-layouts  2.46 us

profile of v1, /device:TPU:0, one launch (start us, length us, event | category | flops | bytes accessed | tf_op | source)
XLA Modules:
  0.0 78.0 jit_solution(2720643722645016582)
XLA Ops:
  1.9 73.6 %whole.1 = (f32[32,32]{1,0:T(8,128)}, f32[2]{0:T(128)}) custom-call(s32[4,4]{1,0:T(4,128)} %pair_hbm.1, s32[2]{0:T(128)} %lengths_hbm.1, s32[1]{0:T(128)S(6)} %copy.17.len_hbm, f32[1]{0:T(128)S(6)} %copy.18.b4_hbm, f32[3,3,32]{2,1,0:T(4,128)} %w1_hbm.1, f32[1,32]{1,0:T(1,128)} %bitcast.20, bf16[9,32,64]{2,1,0:T(8,128)(2,1)} %bitcast.19, f32[1,64]{1,0:T(1,128)} %bitcast.21, ...), custom_call_target="tpu_custom_call" | custom-call | tf_op jit(solution)/shard_map/whole/pallas_call | solution.py:581
  75.6 1.3 %copy.19 = f32[32,32]{1,0:T(8,128)} copy(f32[32,32]{1,0:T(8,128)} %get-tuple-element.4) | data formatting | bytes 8192
  76.9 1.1 %copy.20 = f32[2]{0:T(128)} copy(f32[2]{0:T(128)} %get-tuple-element.5) | data formatting | bytes 16

commit v2 on v1

--- a/solution.py
+++ b/solution.py
@@ -26,30 +26,34 @@
     return [tuple(span) for span in found]
 
 
-def plan(chunks, frames, tiles, last):
+def plan(stages, chunks, frames, tiles):
     side = tiles + 4
     width = frames // chunks
-
-    def early(frame):
-        chunk = chunks - 1 if frame < 0 else 0 if frame >= frames else frame // width
-        return chunk != last
-
-    ready = []
-    for j in range(side):
-        ready.append(all(early(4 * (j - 2) + k) for k in range(-1, 5)))
-    passes = [[ready], [[not flag for flag in ready]]]
-    for layer in (1, 2):
-        wanted = [layer <= j < side - layer for j in range(side)]
-        before = passes[0][-1]
-        now = [wanted[j] and all(before[j + k] for k in (-1, 0, 1)) for j in range(1, side - 1)]
-        now = [False] + now + [False]
-        passes[0].append(now)
-        passes[1].append([wanted[j] and not now[j] for j in range(side)])
-    return [[spans(flags) for flags in one] for one in passes]
-
-
-def chunk_order(chunks, k):
-    return k // 2 + (k % 2) * (chunks - 1 - 2 * (k // 2))
+    here, finished, work = set(), [[False] * side for _ in range(3)], []
+    for stage in stages:
+        here |= set(stage)
+        ready = []
+        for j in range(side):
+            known = True
+            for k in range(-1, 5):
+                frame = 4 * (j - 2) + k
+                outside = chunks - 1 if frame < 0 else 0
+                known &= (frame // width if 0 <= frame < frames else outside) in here
+            ready.append(known)
+        layers = []
+        for layer in range(3):
+            if layer:
+                edge = [False] * layer
+                ready = [all(ready[j - 1 : j + 2]) for j in range(layer, side - layer)]
+                ready = edge + ready + edge
+            layers.append(spans([now and not was for now, was in zip(ready, finished[layer])]))
+            finished[layer] = ready
+        work.append(layers)
+    return work
+
+
+def chunk_order(chunks):
+    return [k // 2 if k % 2 == 0 else chunks - 1 - k // 2 for k in range(chunks)]
 
 
 def whole_kernel(
@@ -61,14 +65,15 @@
     q_buf, r_own, r_far, acc, sims_buf, map_buf, z_buf, x_buf, first_buf, second_buf,
     w1_rep, w1_flat, w1_full, w2_full, w3_full, b1_full, b2_full, score_buf, peaks_buf,
     small_sem, q_sem, own_sem, send_o, recv_o, send_x, recv_x, send_s, recv_s, send_h, recv_h,
-    send_p, recv_p,
+    send_p, recv_p, far_sem,
 ):
     regions, shard, depth = r_hbm.shape
     frames = q_hbm.shape[0] // regions
     chunks = shard // GROUP
     width = GROUP * 2 * chips
     tiles = frames // 4
-    last = chunk_order(chunks, chunks - 1)
+    order = chunk_order(chunks)
+    last = order[-1]
     me = lax.axis_index("qry")
     chip = me // 2
     core = me % 2
@@ -145,38 +150,53 @@
         own_copy(g).start()
     map_buf[...] = jnp.zeros_like(map_buf)
     barrier = pltpu.get_barrier_semaphore()
-
-    def greet(k, carry):
-        peer = (mine + k) % peers
-        device = {"qry": peer // others, "ref": peer % others}
+    for k in range(1, senders):
+        device = {"qry": (me + k) % senders}
         pl.semaphore_signal(barrier, inc=1, device_id=device, device_id_type=MESH)
-        return carry
-
-    lax.fori_loop(1, peers, greet, 0)
+
+    def tell_columns(semaphore):
+        for move, there in ((-1, col > 0), (1, col < others - 1)):
+
+            @pl.when(there)
+            def _():
+                pl.semaphore_signal(
+                    semaphore, inc=1, device_id={"ref": col + move}, device_id_type=MESH
+                )
+
+    columns_near = jnp.where(col > 0, 1, 0) + jnp.where(col < others - 1, 1, 0)
+    tell_columns(barrier)
+    pl.semaphore_wait(barrier, senders - 1 + columns_near)
+
+    def enqueue(lo, hi):
+        for k in range(lo, min(hi, chunks * pieces)):
+            to_right(0, order[k // pieces], k % pieces).start()
+
+    enqueue(0, 3 * pieces // 2)
+    for g in range(chunks):
+        own_to_sibling(g).start()
+    rounds = others - 1
+    if rounds:
+        tell_columns(far_sem.at[0])
+
+    def next_round(k):
+        if k < rounds:
+            pl.semaphore_wait(far_sem.at[k], columns_near)
+            if k + 1 < rounds:
+                tell_columns(far_sem.at[k + 1])
+
     for copy in smalls:
         copy.start()
-    pl.semaphore_wait(barrier, peers - 1)
-
-    def start_sends(k, carry):
-        g = chunk_order(chunks, k)
-        for p in range(pieces):
-            to_right(0, g, p).start()
-        return carry
-
-    lax.fori_loop(0, chunks, start_sends, 0)
-    for g in range(chunks):
-        own_to_sibling(g).start()
-
     z_buf[...] = jnp.zeros_like(z_buf)
     first_buf[...] = jnp.zeros_like(first_buf)
     second_buf[...] = jnp.zeros_like(second_buf)
-    peaks_buf[mine] = jnp.zeros(peaks_buf.shape[1:], jnp.float32)
+    next_round(0)
     for copy in smalls:
         copy.wait()
     build_weights(
         w1_ref, w2_ref, w3_ref, b1_ref, b2_ref, w1_rep, w1_flat, w1_full, w2_full, w3_full,
         b1_full, b2_full,
     )
+    next_round(1)
     factor = pair_ref[me, col].astype(jnp.float32) * scale
 
     def similar(product, blocks):
@@ -208,6 +228,8 @@
         return carry
 
     lax.fori_loop(0, 2, near_side, 0)
+    for k in range(2, rounds):
+        next_round(k)
 
     def sources(step):
         origin = (chip + chips - 1 - step) % chips
@@ -230,18 +252,6 @@
         total = similar(product, 2)
         for k, source in enumerate(sources(step)):
             sims_buf[source, rows_of(g)] = total[k]
-
-    def middle(k, carry):
-        g = chunk_order(chunks, k)
-        for step in range(chips - 1):
-            for p in range(pieces):
-                arrive(step, g, p)
-            for p in range(pieces):
-                to_sibling(step, g, p).wait_recv()
-            keep(step, g, part(step, g, 0, pieces))
-        return carry
-
-    lax.fori_loop(0, chunks - 1, middle, 0)
 
     def reachable(move_q, move_r):
         fits = (me + move_q >= 0) & (me + move_q < senders)
@@ -267,51 +277,65 @@
     moves += [(q, r, 0 if r < 0 else chunks - 1) for r in (-1, 1) for q in (-1, 1, 0)]
     moves = list(enumerate(moves))
 
-    def spread(done):
-        for g in done:
-            for b in range(senders):
-                rows = pl.ds(HALO + g * width + b, GROUP, stride=senders)
-                map_buf.at[1][rows, :] = sims_buf[b, g * GROUP : (g + 1) * GROUP]
-        now = [(k, q, r, g) for k, (q, r, g) in moves if g in done]
-        for k, q, r, g in now:
-
-            @pl.when(reachable(q, r))
-            def _():
-                halo_copy(k, q, r, g).start()
-
-        for k, q, r, g in now:
-
-            @pl.when(reachable(-q, -r))
-            def _():
-                halo_copy(k, q, r, g).wait_recv()
+    def spread(g):
+        for b in range(senders):
+            rows = pl.ds(HALO + g * width + b, GROUP, stride=senders)
+            map_buf.at[1][rows, :] = sims_buf[b, g * GROUP : (g + 1) * GROUP]
+        for k, (q, r, source) in moves:
+            if source == g:
+
+                @pl.when(reachable(q, r))
+                def _():
+                    halo_copy(k, q, r, g).start()
+
+    def halos(stage):
+        for k, (q, r, g) in moves:
+            if g in stage:
+
+                @pl.when(reachable(-q, -r))
+                def _():
+                    halo_copy(k, q, r, g).wait_recv()
 
     where = (me * tiles, col * tiles, senders * tiles, others * tiles)
-    before, after = plan(chunks, frames, tiles, last)
-
-    def network(layers):
-        for lo, hi in layers[0]:
+    stages = (order[: max(chunks - 2, 0)], order[max(chunks - 2, 0) : chunks - 1], [last])
+    work = plan(stages, chunks, frames, tiles)
+
+    def network(k):
+        halos(stages[k])
+        for lo, hi in work[k][0]:
             conv1(lo, hi, where, map_buf, w1_full, b1_full, z_buf, x_buf, first_buf)
-        for lo, hi in layers[1]:
+        for lo, hi in work[k][1]:
             conv2(lo, hi, where, w2_full, b2_full, first_buf, second_buf)
-        for lo, hi in layers[2]:
+        for lo, hi in work[k][2]:
             score_buf[lo:hi, :PITCH] = conv3(lo, hi, w3_full, b3_ref, w4_ref, second_buf)
 
-    if chunks > 1:
-        spread([g for g in range(chunks) if g != last])
-        network(before)
+    for k, g in enumerate(order[:-1]):
+        for step in range(chips - 1):
+            for p in range(pieces):
+                arrive(step, g, p)
+            for p in range(pieces):
+                to_sibling(step, g, p).wait_recv()
+            keep(step, g, part(step, g, 0, pieces))
+        spread(g)
+        enqueue((2 * k + 3) * pieces // 2, (2 * k + 5) * pieces // 2)
+    network(0)
 
     for step in range(chips - 1):
-        for p in range(pieces):
-            arrive(step, last, p)
-            to_sibling(step, last, p).wait_recv()
-            if p == 0:
-                acc[...] = part(step, last, p, p + 1)
-            elif p < pieces - 1:
-                acc[...] += part(step, last, p, p + 1)
+        for lo, hi in ((0, pieces - 3), (pieces - 3, pieces - 1), (pieces - 1, pieces)):
+            for p in range(lo, hi):
+                arrive(step, last, p)
+            for p in range(lo, hi):
+                to_sibling(step, last, p).wait_recv()
+            if lo == 0:
+                acc[...] = part(step, last, lo, hi)
+                if step == 0:
+                    network(1)
+            elif hi < pieces:
+                acc[...] += part(step, last, lo, hi)
             else:
-                keep(step, last, acc[...] + part(step, last, p, p + 1))
-    spread([last])
-    network(after)
+                keep(step, last, acc[...] + part(step, last, lo, hi))
+    spread(last)
+    network(2)
 
     scores = score_buf[...] + b4_ref[0]
     slot_f = lax.broadcasted_iota(jnp.int32, scores.shape, 0)
@@ -539,12 +563,11 @@
     query_mat = jnp.transpose(query_feats, (1, 0, 2)).reshape(regions * frames, depth)
     ref_mat = jnp.transpose(ref_feats, (1, 2, 0, 3)).reshape(regions, -1, depth)
     videos = lengths.shape[0]
-    video_rows = -(-videos // 8) * 8
     shard = ref_mat.shape[1]
     chunks = shard // GROUP
     chips = senders // 2
     steps = max(1, chips - 1)
-    cuts = [0, depth * 9 // 15 // 128 * 128, depth * 13 // 15 // 128 * 128, depth]
+    cuts = [depth * k // 6 // 128 * 128 for k in range(7)]
     pieces = len(cuts) - 1
     tiles = frames // 4
     side = tiles + 4
@@ -552,7 +575,7 @@
     scale = 1.0 / (regions * math.sqrt(depth))
     vmem = pl.BlockSpec(memory_space=pltpu.VMEM)
     smem = pl.BlockSpec(memory_space=pltpu.SMEM)
-    hbm = pl.BlockSpec(memory_space=pl.ANY)
+    hbm = pl.BlockSpec(memory_space=pltpu.HBM)
     dma = pltpu.SemaphoreType.DMA
     f32, bf16 = jnp.float32, jnp.bfloat16
     operands = (
@@ -605,7 +628,7 @@
             pltpu.VMEM((1, 128), f32),
             pltpu.VMEM((1, 128), f32),
             pltpu.VMEM((-(-side // 8) * 8, 128), f32),
-            pltpu.VMEM((senders * others, video_rows, 128), f32),
+            pltpu.VMEM((senders * others, videos, 128), f32),
             dma((11,)),
             dma((regions,)),
             dma((chunks,)),
@@ -619,6 +642,7 @@
             dma((2 * chunks + 6,)),
             dma((senders * others,)),
             dma((senders * others,)),
+            pltpu.SemaphoreType.REGULAR((max(1, others - 1),)),
         ],
         compiler_params=pltpu.CompilerParams(
             collective_id=0, has_side_effects=True, vmem_limit_bytes=56 << 20

time: 78.3 us -> 74.2 us (0.948)
  Pallas kernels: 73.6 us -> 69.5 us
    pallas_call x1, Pallas kernels: 73.6 us -> 69.5 us  [body(): pl.pallas_call(functools.partial(whole_kernel, chips, others, scale, cuts...]
where the time goes in v2:
time: 74.2 us; the launch traced here: 73.9 us
  Pallas kernels  69.5 us (94%)
  local copies, waits for them, and re-layouts  2.46 us (3%)
  between operations  1.94 us (3%)
    pallas_call x1, Pallas kernels, body(): pl.pallas_call(functools.partial(whole_kernel, chips, others, scale, cuts...  69.5 us
    unnamed x2, local copies, waits for them, and re-layouts  2.46 us

profile of v2, /device:TPU:0, one launch (start us, length us, event | category | flops | bytes accessed | tf_op | source)
XLA Modules:
  0.0 73.9 jit_solution(6356749319929469950)
XLA Ops:
  1.9 69.5 %whole.1 = (f32[32,32]{1,0:T(8,128)}, f32[2]{0:T(128)}) custom-call(s32[4,4]{1,0:T(4,128)} %pair_hbm.1, s32[2]{0:T(128)} %lengths_hbm.1, s32[1]{0:T(128)S(6)} %copy.17.len_hbm, f32[1]{0:T(128)S(6)} %copy.18.b4_hbm, f32[3,3,32]{2,1,0:T(4,128)} %w1_hbm.1, f32[1,32]{1,0:T(1,128)} %bitcast.20, bf16[9,32,64]{2,1,0:T(8,128)(2,1)} %bitcast.19, f32[1,64]{1,0:T(1,128)} %bitcast.21, ...), custom_call_target="tpu_custom_call" | custom-call | tf_op jit(solution)/shard_map/whole/pallas_call | solution.py:604
  71.4 1.3 %copy.19 = f32[32,32]{1,0:T(8,128)} copy(f32[32,32]{1,0:T(8,128)} %get-tuple-element.4) | data formatting | bytes 8192
  72.8 1.1 %copy.20 = f32[2]{0:T(128)} copy(f32[2]{0:T(128)} %get-tuple-element.5) | data formatting | bytes 16

commit v3 on v2

--- a/solution.py
+++ b/solution.py
@@ -171,7 +171,9 @@
         for k in range(lo, min(hi, chunks * pieces)):
             to_right(0, order[k // pieces], k % pieces).start()
 
-    enqueue(0, 3 * pieces // 2)
+    limits = [(chunks - 1) * pieces - 1] * chunks + [chunks * pieces - 2, chunks * pieces]
+    limits = [max(limit, 0) for limit in limits[-chunks:]] if chunks > 1 else [pieces]
+    enqueue(0, limits[0])
     for g in range(chunks):
         own_to_sibling(g).start()
     rounds = others - 1
@@ -317,17 +319,19 @@
                 to_sibling(step, g, p).wait_recv()
             keep(step, g, part(step, g, 0, pieces))
         spread(g)
-        enqueue((2 * k + 3) * pieces // 2, (2 * k + 5) * pieces // 2)
+        enqueue(limits[k], limits[k + 1])
     network(0)
 
     for step in range(chips - 1):
         for lo, hi in ((0, pieces - 3), (pieces - 3, pieces - 1), (pieces - 1, pieces)):
             for p in range(lo, hi):
-                arrive(step, last, p)
+                if lo == 0 or p > pieces - 3:
+                    arrive(step, last, p)
             for p in range(lo, hi):
                 to_sibling(step, last, p).wait_recv()
             if lo == 0:
                 acc[...] = part(step, last, lo, hi)
+                arrive(step, last, pieces - 3)
                 if step == 0:
                     network(1)
             elif hi < pieces:
@@ -604,8 +608,8 @@
     scores, totals = pl.pallas_call(
         functools.partial(whole_kernel, chips, others, scale, cuts),
         out_shape=(
-            jax.ShapeDtypeStruct((tiles, tiles), f32),
-            jax.ShapeDtypeStruct((videos,), f32),
+            pltpu.VMEM((tiles, tiles), f32),
+            pltpu.SMEM((videos,), f32),
         ),
         in_specs=[hbm] * len(operands),
         out_specs=(vmem, smem),

time: 74.2 us -> 70.3 us (0.947)
  Pallas kernels: 69.5 us -> 66.9 us
  local copies, waits for them, and re-layouts: 2.46 us -> 1.12 us
    pallas_call x1, Pallas kernels: 69.5 us -> 66.9 us  [body(): pl.pallas_call(functools.partial(whole_kernel, chips, others, scale, cuts...]
    unnamed x2, local copies, waits for them, and re-layouts: 2.46 us -> 1.12 us
where the time goes in v3:
time: 70.3 us; the launch traced here: 70.2 us
  Pallas kernels  66.9 us (95%)
  between operations  2.1 us (3%)
  local copies, waits for them, and re-layouts  1.12 us (2%)
    pallas_call x1, Pallas kernels, body(): pl.pallas_call(functools.partial(whole_kernel, chips, others, scale, cuts...  66.9 us

profile of v3, /device:TPU:0, one launch (start us, length us, event | category | flops | bytes accessed | tf_op | source)
XLA Modules:
  0.0 70.2 jit_solution(8391009844493079576)
XLA Ops:
  1.9 66.9 %whole.1 = (f32[32,32]{1,0:T(8,128)S(1)}, f32[2]{0:T(128)S(4)}) custom-call(s32[4,4]{1,0:T(4,128)} %pair_hbm.1, s32[2]{0:T(128)} %lengths_hbm.1, s32[1]{0:T(128)S(6)} %copy.19.len_hbm, f32[1]{0:T(128)S(6)} %copy.20.b4_hbm, f32[3,3,32]{2,1,0:T(4,128)} %w1_hbm.1, f32[1,32]{1,0:T(1,128)} %bitcast.20, bf16[9,32,64]{2,1,0:T(8,128)(2,1)} %bitcast.19, ...), custom_call_target="tpu_custom_call" | custom-call | tf_op jit(solution)/shard_map/whole/pallas_call | solution.py:608
  68.9 0.6 copy.17
  69.5 0.5 copy.18

commit v4 on v3

--- a/solution.py
+++ b/solution.py
@@ -144,10 +144,6 @@
             device_id_type=MESH,
         )
 
-    for k in range(regions):
-        q_copy(k).start()
-    for g in range(chunks):
-        own_copy(g).start()
     map_buf[...] = jnp.zeros_like(map_buf)
     barrier = pltpu.get_barrier_semaphore()
     for k in range(1, senders):
@@ -173,9 +169,14 @@
 
     limits = [(chunks - 1) * pieces - 1] * chunks + [chunks * pieces - 2, chunks * pieces]
     limits = [max(limit, 0) for limit in limits[-chunks:]] if chunks > 1 else [pieces]
-    enqueue(0, limits[0])
+    enqueue(0, min(pieces, limits[0]))
+    for k in range(regions):
+        q_copy(k).start()
+    for g in range(chunks):
+        own_copy(g).start()
     for g in range(chunks):
         own_to_sibling(g).start()
+    enqueue(min(pieces, limits[0]), limits[0])
     rounds = others - 1
     if rounds:
         tell_columns(far_sem.at[0])
@@ -313,31 +314,35 @@
 
     for k, g in enumerate(order[:-1]):
         for step in range(chips - 1):
-            for p in range(pieces):
-                arrive(step, g, p)
-            for p in range(pieces):
-                to_sibling(step, g, p).wait_recv()
-            keep(step, g, part(step, g, 0, pieces))
+            for lo, hi in ((0, pieces - 2), (pieces - 2, pieces)):
+                for p in range(lo, hi):
+                    arrive(step, g, p)
+                for p in range(lo, hi):
+                    to_sibling(step, g, p).wait_recv()
+                if lo == 0:
+                    acc[...] = part(step, g, lo, hi)
+                else:
+                    keep(step, g, acc[...] + part(step, g, lo, hi))
         spread(g)
         enqueue(limits[k], limits[k + 1])
     network(0)
 
+    def settle(step, lo, hi):
+        for p in range(lo, hi):
+            to_sibling(step, last, p).wait_recv()
+        return part(step, last, lo, hi)
+
     for step in range(chips - 1):
-        for lo, hi in ((0, pieces - 3), (pieces - 3, pieces - 1), (pieces - 1, pieces)):
-            for p in range(lo, hi):
-                if lo == 0 or p > pieces - 3:
-                    arrive(step, last, p)
-            for p in range(lo, hi):
-                to_sibling(step, last, p).wait_recv()
-            if lo == 0:
-                acc[...] = part(step, last, lo, hi)
-                arrive(step, last, pieces - 3)
-                if step == 0:
-                    network(1)
-            elif hi < pieces:
-                acc[...] += part(step, last, lo, hi)
-            else:
-                keep(step, last, acc[...] + part(step, last, lo, hi))
+        for p in range(pieces - 3):
+            arrive(step, last, p)
+        acc[...] = settle(step, 0, pieces - 3)
+        arrive(step, last, pieces - 3)
+        if step == 0:
+            network(1)
+        arrive(step, last, pieces - 2)
+        arrive(step, last, pieces - 1)
+        acc[...] += settle(step, pieces - 3, pieces - 1)
+        keep(step, last, acc[...] + settle(step, pieces - 1, pieces))
     spread(last)
     network(2)
 
@@ -354,14 +359,19 @@
         )
         begin = end
 
+    flip = 2 * col // others
+
     def peak_copy(k):
-        peer = (mine + k) % peers
-        return pltpu.make_async_remote_copy(
+        move = k % senders
+        away = k // senders
+        peer_q = (me + move) % senders
+        peer_r = (1 - flip) * (others - 1 - away) + flip * away
+        return peer_q, peer_r, pltpu.make_async_remote_copy(
             src_ref=peaks_buf.at[mine],
             dst_ref=peaks_buf.at[mine],
             send_sem=send_p.at[k],
             recv_sem=recv_p.at[mine],
-            device_id={"qry": peer // others, "ref": peer % others},
+            device_id={"qry": peer_q, "ref": peer_r},
             device_id_type=MESH,
         )
 
@@ -378,10 +388,15 @@
         return carry
 
     def peak_start(k, carry):
-        peak_copy(k).start()
+        peer_q, peer_r, copy = peak_copy(k)
+
+        @pl.when((peer_q != me) | (peer_r != col))
+        def _():
+            copy.start()
+
         return carry
 
-    lax.fori_loop(1, peers, peak_start, 0)
+    lax.fori_loop(0, peers, peak_start, 0)
     scores_ref[...] = jnp.transpose(scores)[2 : 2 + tiles, 2 : 2 + tiles]
 
     def drain(g, carry):
@@ -411,10 +426,15 @@
         totals_ref[v] = jnp.sum(total[v : v + 1])
 
     def peak_drain(k, carry):
-        peak_copy(k).wait_send()
+        peer_q, peer_r, copy = peak_copy(k)
+
+        @pl.when((peer_q != me) | (peer_r != col))
+        def _():
+            copy.wait_send()
+
         return carry
 
-    lax.fori_loop(1, peers, peak_drain, 0)
+    lax.fori_loop(0, peers, peak_drain, 0)
 
 
 def build_weights(

time: 70.3 us -> 69.7 us (level)
  no operation moved by 1% of the time
where the time goes in v4:
time: 69.7 us; the launch traced here: 69.5 us
  Pallas kernels  66.3 us (95%)
  between operations  2.1 us (3%)
  local copies, waits for them, and re-layouts  1.12 us (2%)
    pallas_call x1, Pallas kernels, body(): pl.pallas_call(functools.partial(whole_kernel, chips, others, scale, cuts...  66.3 us

profile of v4, /device:TPU:0, one launch (start us, length us, event | category | flops | bytes accessed | tf_op | source)
XLA Modules:
  0.0 69.5 jit_solution(16196644177062125926)
XLA Ops:
  1.9 66.3 %whole.1 = (f32[32,32]{1,0:T(8,128)S(1)}, f32[2]{0:T(128)S(4)}) custom-call(s32[4,4]{1,0:T(4,128)} %pair_hbm.1, s32[2]{0:T(128)} %lengths_hbm.1, s32[1]{0:T(128)S(6)} %copy.19.len_hbm, f32[1]{0:T(128)S(6)} %copy.20.b4_hbm, f32[3,3,32]{2,1,0:T(4,128)} %w1_hbm.1, f32[1,32]{1,0:T(1,128)} %bitcast.20, bf16[9,32,64]{2,1,0:T(8,128)(2,1)} %bitcast.19, ...), custom_call_target="tpu_custom_call" | custom-call | tf_op jit(solution)/shard_map/whole/pallas_call | solution.py:628
  68.2 0.6 copy.17
  68.8 0.5 copy.18

commit v5 on v4

--- a/solution.py
+++ b/solution.py
@@ -63,7 +63,7 @@
     scores_ref, totals_ref,
     pair_ref, lengths_ref, len_ref, b4_ref, w1_ref, b1_ref, w2_ref, b2_ref, w3_ref, b3_ref, w4_ref,
     q_buf, r_own, r_far, acc, sims_buf, map_buf, z_buf, x_buf, first_buf, second_buf,
-    w1_rep, w1_flat, w1_full, w2_full, w3_full, b1_full, b2_full, score_buf, peaks_buf,
+    w1_rep, w1_flat, w1_full, w2_full, w3_full, b1_full, b2_full, pick_full, score_buf, peaks_buf,
     small_sem, q_sem, own_sem, send_o, recv_o, send_x, recv_x, send_s, recv_s, send_h, recv_h,
     send_p, recv_p, far_sem,
 ):
@@ -103,22 +103,35 @@
     def rows_of(g):
         return pl.ds(pl.multiple_of(g * GROUP, GROUP), GROUP)
 
+    def batches(g):
+        steps = (0, pieces - 3, pieces - 1, pieces) if g == last else (0, pieces - 2, pieces)
+        return list(zip(steps[:-1], steps[1:]))
+
+    def batch(g, p):
+        return [lo <= p < hi for lo, hi in batches(g)].index(True)
+
+    def all_of(ref, device, send_sem, recv_sem):
+        return pltpu.make_async_remote_copy(
+            src_ref=ref, dst_ref=ref, send_sem=send_sem, recv_sem=recv_sem,
+            device_id=device, device_id_type=MESH,
+        )
+
     def own_copy(g):
-        return pltpu.make_async_copy(r_hbm.at[:, rows_of(g)], r_own.at[0, g], own_sem.at[g])
+        return pltpu.make_async_copy(r_hbm.at[:, rows_of(g)], r_own.at[0, g], own_sem)
 
     def own_to_sibling(g):
         return pltpu.make_async_remote_copy(
             src_ref=r_hbm.at[:, rows_of(g)],
             dst_ref=r_own.at[1, g],
-            send_sem=send_o.at[g],
-            recv_sem=recv_o.at[g],
+            send_sem=send_o,
+            recv_sem=recv_o,
             device_id={"qry": sibling},
             device_id_type=MESH,
         )
 
     def q_copy(k):
         rows = pl.ds(k * frames, frames)
-        return pltpu.make_async_copy(q_hbm.at[rows], q_buf.at[rows], q_sem.at[k])
+        return pltpu.make_async_copy(q_hbm.at[rows], q_buf.at[rows], q_sem)
 
     def to_right(step, g, p):
         if step == 0:
@@ -128,7 +141,7 @@
         return pltpu.make_async_remote_copy(
             src_ref=source,
             dst_ref=r_far.at[step, g, 0, :, :, piece(p)],
-            send_sem=send_x.at[step, g, p],
+            send_sem=send_x.at[step],
             recv_sem=recv_x.at[step, g, p],
             device_id={"qry": right},
             device_id_type=MESH,
@@ -138,8 +151,8 @@
         return pltpu.make_async_remote_copy(
             src_ref=r_far.at[step, g, 0, :, :, piece(p)],
             dst_ref=r_far.at[step, g, 1, :, :, piece(p)],
-            send_sem=send_s.at[step, g, p],
-            recv_sem=recv_s.at[step, g, p],
+            send_sem=send_s.at[step],
+            recv_sem=recv_s.at[step, g, batch(g, p)],
             device_id={"qry": sibling},
             device_id_type=MESH,
         )
@@ -197,7 +210,7 @@
         copy.wait()
     build_weights(
         w1_ref, w2_ref, w3_ref, b1_ref, b2_ref, w1_rep, w1_flat, w1_full, w2_full, w3_full,
-        b1_full, b2_full,
+        b1_full, b2_full, pick_full,
     )
     next_round(1)
     factor = pair_ref[me, col].astype(jnp.float32) * scale
@@ -216,16 +229,13 @@
         )
         return similar(product, chunks).reshape(shard, frames)
 
-    for k in range(regions):
-        q_copy(k).wait()
-    for g in range(chunks):
-        own_copy(g).wait()
+    pltpu.make_async_copy(q_hbm, q_buf, q_sem).wait()
+    pltpu.make_async_copy(r_own.at[0], r_own.at[0], own_sem).wait()
 
     def near_side(side, carry):
         @pl.when(side == 1)
         def _():
-            for g in range(chunks):
-                own_to_sibling(g).wait_recv()
+            all_of(r_own.at[1], {"qry": sibling}, send_o, recv_o).wait_recv()
 
         sims_buf[chip * 2 + side * (1 - core) + (1 - side) * core] = near(side)
         return carry
@@ -243,6 +253,14 @@
         to_sibling(step, g, p).start()
         if step < chips - 2:
             to_right(step + 1, g, p).start()
+
+    def settle(step, g, lo, hi):
+        columns = pl.ds(cuts[lo], cuts[hi] - cuts[lo])
+        all_of(
+            r_far.at[step, g, 1, :, :, columns], {"qry": sibling}, send_s.at[step],
+            recv_s.at[step, g, batch(g, lo)],
+        ).wait_recv()
+        return part(step, g, lo, hi)
 
     def part(step, g, first_piece, final_piece):
         columns = pl.ds(cuts[first_piece], cuts[final_piece] - cuts[first_piece])
@@ -306,7 +324,7 @@
     def network(k):
         halos(stages[k])
         for lo, hi in work[k][0]:
-            conv1(lo, hi, where, map_buf, w1_full, b1_full, z_buf, x_buf, first_buf)
+            conv1(lo, hi, where, map_buf, pick_full, w1_full, b1_full, z_buf, x_buf, first_buf)
         for lo, hi in work[k][1]:
             conv2(lo, hi, where, w2_full, b2_full, first_buf, second_buf)
         for lo, hi in work[k][2]:
@@ -314,35 +332,28 @@
 
     for k, g in enumerate(order[:-1]):
         for step in range(chips - 1):
-            for lo, hi in ((0, pieces - 2), (pieces - 2, pieces)):
+            for lo, hi in batches(g):
                 for p in range(lo, hi):
                     arrive(step, g, p)
-                for p in range(lo, hi):
-                    to_sibling(step, g, p).wait_recv()
                 if lo == 0:
-                    acc[...] = part(step, g, lo, hi)
+                    acc[...] = settle(step, g, lo, hi)
                 else:
-                    keep(step, g, acc[...] + part(step, g, lo, hi))
+                    keep(step, g, acc[...] + settle(step, g, lo, hi))
         spread(g)
         enqueue(limits[k], limits[k + 1])
     network(0)
 
-    def settle(step, lo, hi):
-        for p in range(lo, hi):
-            to_sibling(step, last, p).wait_recv()
-        return part(step, last, lo, hi)
-
     for step in range(chips - 1):
         for p in range(pieces - 3):
             arrive(step, last, p)
-        acc[...] = settle(step, 0, pieces - 3)
+        acc[...] = settle(step, last, 0, pieces - 3)
         arrive(step, last, pieces - 3)
         if step == 0:
             network(1)
         arrive(step, last, pieces - 2)
         arrive(step, last, pieces - 1)
-        acc[...] += settle(step, pieces - 3, pieces - 1)
-        keep(step, last, acc[...] + settle(step, pieces - 1, pieces))
+        acc[...] += settle(step, last, pieces - 3, pieces - 1)
+        keep(step, last, acc[...] + settle(step, last, pieces - 1, pieces))
     spread(last)
     network(2)
 
@@ -369,23 +380,11 @@
         return peer_q, peer_r, pltpu.make_async_remote_copy(
             src_ref=peaks_buf.at[mine],
             dst_ref=peaks_buf.at[mine],
-            send_sem=send_p.at[k],
-            recv_sem=recv_p.at[mine],
+            send_sem=send_p,
+            recv_sem=recv_p,
             device_id={"qry": peer_q, "ref": peer_r},
             device_id_type=MESH,
         )
-
-    def peak_wait(k, carry):
-        peer = (mine + k) % peers
-        pltpu.make_async_remote_copy(
-            src_ref=peaks_buf.at[peer],
-            dst_ref=peaks_buf.at[peer],
-            send_sem=send_p.at[k],
-            recv_sem=recv_p.at[peer],
-            device_id={"qry": peer // others, "ref": peer % others},
-            device_id_type=MESH,
-        ).wait_recv()
-        return carry
 
     def peak_start(k, carry):
         peer_q, peer_r, copy = peak_copy(k)
@@ -399,22 +398,21 @@
     lax.fori_loop(0, peers, peak_start, 0)
     scores_ref[...] = jnp.transpose(scores)[2 : 2 + tiles, 2 : 2 + tiles]
 
-    def drain(g, carry):
-        own_to_sibling(g).wait_send()
-        for step in range(chips - 1):
-            for p in range(pieces):
-                to_right(step, g, p).wait_send()
-                to_sibling(step, g, p).wait_send()
-        return carry
-
-    lax.fori_loop(0, chunks, drain, 0)
+    all_of(r_own.at[1], {"qry": sibling}, send_o, recv_o).wait_send()
+    for step in range(chips - 1):
+        sent = r_far.at[step, :, 0]
+        all_of(sent, {"qry": right}, send_x.at[step], send_x.at[step]).wait_send()
+        all_of(sent, {"qry": sibling}, send_s.at[step], send_s.at[step]).wait_send()
     for k, (q, r, g) in moves:
 
         @pl.when(reachable(q, r))
         def _():
             halo_copy(k, q, r, g).wait_send()
 
-    lax.fori_loop(1, peers, peak_wait, 0)
+    heard = all_of(
+        peaks_buf.at[pl.ds(0, peers - 1)], {"qry": sibling}, send_p, recv_p
+    )
+    heard.wait_recv()
     lane = lax.broadcasted_iota(jnp.int32, peaks_buf.shape[1:], 1)
     total = jnp.zeros(peaks_buf.shape[1:], jnp.float32)
     for s in range(senders):
@@ -425,21 +423,12 @@
     for v in range(lengths_ref.shape[0]):
         totals_ref[v] = jnp.sum(total[v : v + 1])
 
-    def peak_drain(k, carry):
-        peer_q, peer_r, copy = peak_copy(k)
-
-        @pl.when((peer_q != me) | (peer_r != col))
-        def _():
-            copy.wait_send()
-
-        return carry
-
-    lax.fori_loop(0, peers, peak_drain, 0)
+    heard.wait_send()
 
 
 def build_weights(
     w1_ref, w2_ref, w3_ref, b1_ref, b2_ref, w1_rep, w1_flat, w1_full, w2_full, w3_full,
-    b1_full, b2_full,
+    b1_full, b2_full, pick_full,
 ):
     for k in range(4):
         lanes = slice(k * 32, (k + 1) * 32)
@@ -456,13 +445,27 @@
                     at = (a * 2 + b) * 32
                     col = (u * 2 + v) * 128 + at
                     for k in range(9):
-                        row = (2 * a + u + k // 3) * 8 + 2 * b + v + k % 3
-                        w1_flat[row : row + 1, col : col + 32] = w1_rep[k : k + 1, at : at + 32]
+                        rr = 2 * a + u + k // 3
+                        for part in range(2):
+                            row = rr % 2 * 48 + part * 24 + rr // 2 * 8 + 2 * b + v + k % 3
+                            w1_flat[row : row + 1, col : col + 32] = w1_rep[
+                                k : k + 1, at : at + 32
+                            ]
     flat = w1_flat[...]
     high = flat.astype(jnp.bfloat16)
-    w1_full[0:48] = high
-    w1_full[48:96] = high
-    w1_full[96:144] = (flat - high.astype(jnp.float32)).astype(jnp.bfloat16)
+    row = lax.broadcasted_iota(jnp.int32, flat.shape, 0)
+    w1_full[0:128] = high
+    w1_full[128:256] = jnp.where(
+        row % 48 < 24, flat - high.astype(jnp.float32), 0.0
+    ).astype(jnp.bfloat16)
+    frames = pick_full.shape[0] // 3
+    source = lax.broadcasted_iota(jnp.int32, (3 * frames, 128), 0)
+    target = lax.broadcasted_iota(jnp.int32, (3 * frames, 128), 1)
+    begin = 4 * (target % 64) + target // 64 + (frames - 9)
+    for k in range(3):
+        pick_full[:, k * 128 : (k + 1) * 128] = jnp.where(
+            source == begin + 2 * k, 1.0, 0.0
+        ).astype(jnp.bfloat16)
 
     w2_full[...] = jnp.zeros_like(w2_full)
     taps = {(0, 0): 0, (0, 1): 1, (1, 0): 2, (1, 1): -1}
@@ -491,34 +494,32 @@
     return jnp.where(inside, 1.0, 0.0).reshape((hi - lo) * PITCH, 128)
 
 
-def conv1(lo, hi, where, map_ref, w1_full, b1_full, z_buf, x_buf, first_buf):
-    wide, frames = map_ref.shape[1:]
+def conv1(lo, hi, where, map_ref, pick_full, w1_full, b1_full, z_buf, x_buf, first_buf):
+    wide = map_ref.shape[1]
     top = max(0, (4 * lo - 1) // 8 * 8)
     end = min(wide, -(-(4 * hi + 3) // 8) * 8)
-    source = lax.broadcasted_iota(jnp.int32, (3 * frames, 128), 0)
-    target = lax.broadcasted_iota(jnp.int32, (3 * frames, 128), 1)
     whole = jnp.concatenate([map_ref[k, top:end] for k in range(3)], axis=1)
     high = whole.astype(jnp.bfloat16)
     lower = (whole - high.astype(jnp.float32)).astype(jnp.bfloat16)
-    for rr in range(6):
-        pick = jnp.where(source == 4 * target + (frames - 9) + rr, 1.0, 0.0).astype(jnp.bfloat16)
-        for part, value in enumerate((high, lower)):
-            z_buf[part, 8 + top : 8 + end, rr * 128 : (rr + 1) * 128] = jnp.dot(
-                value, pick, preferred_element_type=jnp.float32
-            )
+    for part, value in enumerate((high, lower)):
+        z_buf[part, 8 + top : 8 + end, :] = jnp.dot(
+            value, pick_full[...], preferred_element_type=jnp.float32
+        )
+    blank = jnp.zeros((PITCH, 32), jnp.float32)
     for block in range(lo, hi):
-        pieces = []
-        for part in (0, 1, 0):
-            for rr in range(6):
-                pieces.append(
-                    z_buf[part, 4 * block + 7 : 4 * block + 15, rr * 128 : (rr + 1) * 128]
-                )
-        flat = jnp.concatenate(pieces, axis=0)
-        x_buf[block * PITCH : (block + 1) * PITCH, :] = jnp.transpose(flat)[:PITCH]
-
+        pieces = [
+            z_buf[part, 4 * block + 7 : 4 * block + 15, k * 128 : (k + 1) * 128]
+            for part in range(2)
+            for k in range(3)
+        ]
+        turned = jnp.transpose(jnp.concatenate(pieces, axis=0))
+        x_buf[block * PITCH : (block + 1) * PITCH, :] = jnp.concatenate(
+            [turned[:PITCH], turned[64 : 64 + PITCH], blank], axis=1
+        )
+
+    x = x_buf[lo * PITCH : hi * PITCH].astype(jnp.bfloat16)
     made = jnp.dot(
-        x_buf[lo * PITCH : hi * PITCH].astype(jnp.bfloat16), w1_full[...],
-        preferred_element_type=jnp.float32,
+        jnp.concatenate([x, x], axis=1), w1_full[...], preferred_element_type=jnp.float32
     )
     best = jnp.maximum(
         jnp.maximum(made[:, 0:128], made[:, 128:256]),
@@ -640,32 +641,33 @@
             pltpu.VMEM((2 * regions * GROUP, regions * frames), f32),
             pltpu.VMEM((senders, shard, frames), f32),
             pltpu.VMEM((3, frames + 2 * HALO, frames), f32),
-            pltpu.VMEM((2, frames + 4 * HALO, 768), f32),
-            pltpu.VMEM((rows, 144), f32),
+            pltpu.VMEM((2, frames + 4 * HALO, 384), f32),
+            pltpu.VMEM((rows, 128), f32),
             pltpu.VMEM((rows + 2 * LEAD, 128), f32),
             pltpu.VMEM((rows + 2 * LEAD, 128), f32),
             pltpu.VMEM((16, 128), f32),
-            pltpu.VMEM((48, 512), f32),
-            pltpu.VMEM((144, 512), bf16),
+            pltpu.VMEM((128, 512), f32),
+            pltpu.VMEM((256, 512), bf16),
             pltpu.VMEM((512, 256), bf16),
             pltpu.VMEM((640, 128), bf16),
             pltpu.VMEM((1, 128), f32),
             pltpu.VMEM((1, 128), f32),
+            pltpu.VMEM((3 * frames, 384), bf16),
             pltpu.VMEM((-(-side // 8) * 8, 128), f32),
             pltpu.VMEM((senders * others, videos, 128), f32),
             dma((11,)),
-            dma((regions,)),
-            dma((chunks,)),
-            dma((chunks,)),
-            dma((chunks,)),
+            dma(()),
+            dma(()),
+            dma(()),
+            dma(()),
+            dma((steps,)),
             dma((steps, chunks, pieces)),
-            dma((steps, chunks, pieces)),
-            dma((steps, chunks, pieces)),
-            dma((steps, chunks, pieces)),
+            dma((steps,)),
+            dma((steps, chunks, 3)),
             dma((2 * chunks + 6,)),
             dma((2 * chunks + 6,)),
-            dma((senders * others,)),
-            dma((senders * others,)),
+            dma(()),
+            dma(()),
             pltpu.SemaphoreType.REGULAR((max(1, others - 1),)),
         ],
         compiler_params=pltpu.CompilerParams(

time: 69.7 us -> 68.4 us (0.981)
  Pallas kernels: 66.3 us -> 65 us
    pallas_call x1, Pallas kernels: 66.3 us -> 65 us  [body(): pl.pallas_call(functools.partial(whole_kernel, chips, others, scale, cuts...]
where the time goes in v5:
time: 68.4 us; the launch traced here: 68.2 us
  Pallas kernels  65 us (95%)
  between operations  2.1 us (3%)
  local copies, waits for them, and re-layouts  1.12 us (2%)
    pallas_call x1, Pallas kernels, body(): pl.pallas_call(functools.partial(whole_kernel, chips, others, scale, cuts...  65 us

profile of v5, /device:TPU:0, one launch (start us, length us, event | category | flops | bytes accessed | tf_op | source)
XLA Modules:
  0.0 68.2 jit_solution(487294200813655331)
XLA Ops:
  1.9 65.0 %whole.1 = (f32[32,32]{1,0:T(8,128)S(1)}, f32[2]{0:T(128)S(4)}) custom-call(s32[4,4]{1,0:T(4,128)} %pair_hbm.1, s32[2]{0:T(128)} %lengths_hbm.1, s32[1]{0:T(128)S(6)} %copy.19.len_hbm, f32[1]{0:T(128)S(6)} %copy.20.b4_hbm, f32[3,3,32]{2,1,0:T(4,128)} %w1_hbm.1, f32[1,32]{1,0:T(1,128)} %bitcast.20, bf16[9,32,64]{2,1,0:T(8,128)(2,1)} %bitcast.19, ...), custom_call_target="tpu_custom_call" | custom-call | tf_op jit(solution)/shard_map/whole/pallas_call | solution.py:629
  66.9 0.6 copy.17
  67.5 0.5 copy.18

commit v6 on v5

--- a/solution.py
+++ b/solution.py
@@ -12,6 +12,10 @@
 HALO = 8
 PITCH = 40
 LEAD = 48
+OFF = 4
+EDGES = ((0, 8), (32, 40))
+ALL = ((0, 40),)
+INNER = ((8, 32),)
 GROUP = 8
 NT = (((1,), (1,)), ((), ()))
 
@@ -58,12 +62,12 @@
 
 def whole_kernel(
     chips, others, scale, cuts,
-    pair_hbm, lengths_hbm, len_hbm, b4_hbm, w1_hbm, b1_hbm, w2_hbm, b2_hbm, w3_hbm, b3_hbm,
+    pair_hbm, lengths_hbm, len_ref, b4_ref, w1_hbm, b1_hbm, w2_hbm, b2_hbm, w3_hbm, b3_hbm,
     w4_hbm, q_hbm, r_hbm,
     scores_ref, totals_ref,
-    pair_ref, lengths_ref, len_ref, b4_ref, w1_ref, b1_ref, w2_ref, b2_ref, w3_ref, b3_ref, w4_ref,
+    pair_ref, lengths_ref, w1_ref, b1_ref, w2_ref, b2_ref, w3_ref, b3_ref, w4_ref,
     q_buf, r_own, r_far, acc, sims_buf, map_buf, z_buf, x_buf, first_buf, second_buf,
-    w1_rep, w1_flat, w1_full, w2_full, w3_full, b1_full, b2_full, pick_full, score_buf, peaks_buf,
+    w1_rep, w1_flat, w1_full, w2_full, w3_full, b1_full, b2_full, pick_full, pick_edge, score_buf, peaks_buf,
     small_sem, q_sem, own_sem, send_o, recv_o, send_x, recv_x, send_s, recv_s, send_h, recv_h,
     send_p, recv_p, far_sem,
 ):
@@ -90,7 +94,7 @@
             (
                 (w1_hbm, w1_ref), (b1_hbm, b1_ref), (w2_hbm, w2_ref), (b2_hbm, b2_ref),
                 (w3_hbm, w3_ref), (b3_hbm, b3_ref), (w4_hbm, w4_ref), (pair_hbm, pair_ref),
-                (lengths_hbm, lengths_ref), (len_hbm, len_ref), (b4_hbm, b4_ref),
+                (lengths_hbm, lengths_ref),
             )
         )
     ]
@@ -210,7 +214,7 @@
         copy.wait()
     build_weights(
         w1_ref, w2_ref, w3_ref, b1_ref, b2_ref, w1_rep, w1_flat, w1_full, w2_full, w3_full,
-        b1_full, b2_full, pick_full,
+        b1_full, b2_full, pick_full, pick_edge,
     )
     next_round(1)
     factor = pair_ref[me, col].astype(jnp.float32) * scale
@@ -321,14 +325,24 @@
     stages = (order[: max(chunks - 2, 0)], order[max(chunks - 2, 0) : chunks - 1], [last])
     work = plan(stages, chunks, frames, tiles)
 
+    def convolve(k, parts, pick, groups, kept):
+        for lo, hi in work[k][0]:
+            conv1(
+                lo, hi, groups, parts, where, map_buf, pick, w1_full, b1_full, z_buf, x_buf,
+                first_buf,
+            )
+        for lo, hi in work[k][1]:
+            conv2(lo, hi, groups, where, w2_full, b2_full, first_buf, second_buf)
+        for lo, hi in work[k][2]:
+            found = conv3(lo, hi, kept, w3_full, b3_ref, w4_ref, second_buf)
+            at = 0
+            for t, end in kept:
+                score_buf[lo:hi, t:end] = found[:, at : at + end - t]
+                at += end - t
+
     def network(k):
         halos(stages[k])
-        for lo, hi in work[k][0]:
-            conv1(lo, hi, where, map_buf, pick_full, w1_full, b1_full, z_buf, x_buf, first_buf)
-        for lo, hi in work[k][1]:
-            conv2(lo, hi, where, w2_full, b2_full, first_buf, second_buf)
-        for lo, hi in work[k][2]:
-            score_buf[lo:hi, :PITCH] = conv3(lo, hi, w3_full, b3_ref, w4_ref, second_buf)
+        convolve(k, (0, 1, 2), pick_full, ALL, ALL)
 
     for k, g in enumerate(order[:-1]):
         for step in range(chips - 1):
@@ -355,7 +369,9 @@
         acc[...] += settle(step, last, pieces - 3, pieces - 1)
         keep(step, last, acc[...] + settle(step, last, pieces - 1, pieces))
     spread(last)
-    network(2)
+    convolve(2, (1,), pick_full, ALL, INNER)
+    halos(stages[2])
+    convolve(2, (0, 1, 2), pick_edge, EDGES, EDGES)
 
     scores = score_buf[...] + b4_ref[0]
     slot_f = lax.broadcasted_iota(jnp.int32, scores.shape, 0)
@@ -396,7 +412,7 @@
         return carry
 
     lax.fori_loop(0, peers, peak_start, 0)
-    scores_ref[...] = jnp.transpose(scores)[2 : 2 + tiles, 2 : 2 + tiles]
+    scores_ref[...] = jnp.transpose(scores)[OFF : OFF + tiles, 2 : 2 + tiles]
 
     all_of(r_own.at[1], {"qry": sibling}, send_o, recv_o).wait_send()
     for step in range(chips - 1):
@@ -417,7 +433,8 @@
     total = jnp.zeros(peaks_buf.shape[1:], jnp.float32)
     for s in range(senders):
         best = jnp.max(peaks_buf[s * others : (s + 1) * others], axis=0)
-        counted = (lane >= 2) & (lane < 2 + tiles) & (lane + (s * tiles - 2) < len_ref[0])
+        counted = (lane >= OFF) & (lane < OFF + tiles)
+        counted = counted & (lane + (s * tiles - OFF) < len_ref[0])
         total = total + jnp.where(counted, best, 0.0)
     total = jnp.sum(total, axis=1, keepdims=True) / len_ref[0].astype(jnp.float32)
     for v in range(lengths_ref.shape[0]):
@@ -428,7 +445,7 @@
 
 def build_weights(
     w1_ref, w2_ref, w3_ref, b1_ref, b2_ref, w1_rep, w1_flat, w1_full, w2_full, w3_full,
-    b1_full, b2_full, pick_full,
+    b1_full, b2_full, pick_full, pick_edge,
 ):
     for k in range(4):
         lanes = slice(k * 32, (k + 1) * 32)
@@ -461,9 +478,16 @@
     frames = pick_full.shape[0] // 3
     source = lax.broadcasted_iota(jnp.int32, (3 * frames, 128), 0)
     target = lax.broadcasted_iota(jnp.int32, (3 * frames, 128), 1)
-    begin = 4 * (target % 64) + target // 64 + (frames - 9)
+    begin = 4 * (target % 64 - OFF) + target // 64 + (frames - 1)
     for k in range(3):
         pick_full[:, k * 128 : (k + 1) * 128] = jnp.where(
+            source == begin + 2 * k, 1.0, 0.0
+        ).astype(jnp.bfloat16)
+    at = target % 16
+    at = jnp.where(at < 8, at, at + 24)
+    begin = 4 * (at - OFF) + target // 64 + (frames - 1)
+    for k in range(3):
+        pick_edge[:, k * 128 : (k + 1) * 128] = jnp.where(
             source == begin + 2 * k, 1.0, 0.0
         ).astype(jnp.bfloat16)
 
@@ -486,38 +510,88 @@
     w3_full[576:640, :] = jnp.zeros((64, 128), jnp.bfloat16)
 
 
-def inside_map(lo, hi, where):
-    shape = (hi - lo, PITCH, 128)
+def span_of(groups):
+    return sum(end - t for t, end in groups)
+
+
+def inside_map(lo, hi, groups, where):
+    shape = (hi - lo, span_of(groups), 128)
     at_f = lax.broadcasted_iota(jnp.int32, shape, 0) + (where[1] - 2 + lo)
-    at_p = lax.broadcasted_iota(jnp.int32, shape, 1) + (where[0] - 2)
+    at_p = lax.broadcasted_iota(jnp.int32, shape, 1)
+    if groups == EDGES:
+        at_p = jnp.where(at_p < 8, at_p, at_p + 24)
+    at_p = at_p + (where[0] - OFF)
     inside = (at_f >= 0) & (at_f < where[3]) & (at_p >= 0) & (at_p < where[2])
-    return jnp.where(inside, 1.0, 0.0).reshape((hi - lo) * PITCH, 128)
-
-
-def conv1(lo, hi, where, map_ref, pick_full, w1_full, b1_full, z_buf, x_buf, first_buf):
-    wide = map_ref.shape[1]
+    return jnp.where(inside, 1.0, 0.0).reshape(shape[0] * shape[1], 128)
+
+
+def rows_at(ref, lo, hi, shift, groups):
+    if groups == ALL:
+        return ref[LEAD + lo * PITCH + shift : LEAD + hi * PITCH + shift, :]
+    found = []
+    for block in range(lo, hi):
+        base = LEAD + block * PITCH + shift
+        found += [ref[base + t : base + end, :] for t, end in groups]
+    return jnp.concatenate(found, axis=0)
+
+
+def put_rows(ref, lo, hi, groups, value):
+    if groups == ALL:
+        ref[LEAD + lo * PITCH : LEAD + hi * PITCH, :] = value
+        return
+    at = 0
+    for block in range(lo, hi):
+        base = LEAD + block * PITCH
+        for t, end in groups:
+            ref[base + t : base + end, :] = value[at : at + end - t]
+            at += end - t
+
+
+def conv1(
+    lo, hi, groups, parts, where, map_ref, pick_ref, w1_full, b1_full, z_buf, x_buf, first_buf
+):
+    wide, frames = map_ref.shape[1:]
     top = max(0, (4 * lo - 1) // 8 * 8)
     end = min(wide, -(-(4 * hi + 3) // 8) * 8)
-    whole = jnp.concatenate([map_ref[k, top:end] for k in range(3)], axis=1)
+    whole = [map_ref[k, top:end] for k in parts]
+    whole = jnp.concatenate(whole, axis=1) if len(whole) > 1 else whole[0]
     high = whole.astype(jnp.bfloat16)
     lower = (whole - high.astype(jnp.float32)).astype(jnp.bfloat16)
+    pick = pick_ref[parts[0] * frames : (parts[-1] + 1) * frames]
     for part, value in enumerate((high, lower)):
         z_buf[part, 8 + top : 8 + end, :] = jnp.dot(
-            value, pick_full[...], preferred_element_type=jnp.float32
-        )
-    blank = jnp.zeros((PITCH, 32), jnp.float32)
-    for block in range(lo, hi):
-        pieces = [
-            z_buf[part, 4 * block + 7 : 4 * block + 15, k * 128 : (k + 1) * 128]
-            for part in range(2)
-            for k in range(3)
-        ]
-        turned = jnp.transpose(jnp.concatenate(pieces, axis=0))
-        x_buf[block * PITCH : (block + 1) * PITCH, :] = jnp.concatenate(
-            [turned[:PITCH], turned[64 : 64 + PITCH], blank], axis=1
-        )
-
-    x = x_buf[lo * PITCH : hi * PITCH].astype(jnp.bfloat16)
+            value, pick, preferred_element_type=jnp.float32
+        )
+
+    def window(block, part, k):
+        return z_buf[part, 4 * block + 7 : 4 * block + 15, k * 128 : (k + 1) * 128]
+
+    kinds = [(part, k) for part in range(2) for k in range(3)]
+    if groups == ALL:
+        blank = jnp.zeros((PITCH, 32), jnp.float32)
+        for block in range(lo, hi):
+            turned = jnp.transpose(
+                jnp.concatenate([window(block, *kind) for kind in kinds], axis=0)
+            )
+            x_buf[block * PITCH : (block + 1) * PITCH, :] = jnp.concatenate(
+                [turned[:PITCH], turned[64 : 64 + PITCH], blank], axis=1
+            )
+        x = x_buf[lo * PITCH : hi * PITCH]
+    else:
+        blank = jnp.zeros((64, 32), jnp.float32)
+        place = lax.broadcasted_iota(jnp.int32, (8, 128), 1) % 64 // 16
+        found = []
+        for block in range(lo, hi, 4):
+            pieces = []
+            for kind in kinds:
+                piece = window(block, *kind)
+                for g in range(1, min(4, hi - block)):
+                    piece = jnp.where(place == g, window(block + g, *kind), piece)
+                pieces.append(piece)
+            turned = jnp.transpose(jnp.concatenate(pieces, axis=0))
+            found.append(jnp.concatenate([turned[:64], turned[64:], blank], axis=1))
+        x = jnp.concatenate(found, axis=0)[: (hi - lo) * 16]
+    x = x.astype(jnp.bfloat16)
     made = jnp.dot(
         jnp.concatenate([x, x], axis=1), w1_full[...], preferred_element_type=jnp.float32
     )
@@ -526,56 +600,50 @@
         jnp.maximum(made[:, 256:384], made[:, 384:512]),
     )
     first = jnp.maximum(best + b1_full[...], 0.0)
-    first = jnp.where(inside_map(lo, hi, where) > 0.5, first, 0.0)
-    first = first.astype(jnp.bfloat16).astype(jnp.float32)
-    first_buf[LEAD + lo * PITCH : LEAD + hi * PITCH, :] = first
-
-
-def conv2(lo, hi, where, w2_full, b2_full, first_buf, second_buf):
+    first = first * inside_map(lo, hi, groups, where)
+    put_rows(first_buf, lo, hi, groups, first.astype(jnp.bfloat16).astype(jnp.float32))
+
+
+def conv2(lo, hi, groups, where, w2_full, b2_full, first_buf, second_buf):
     lane = lax.broadcasted_iota(jnp.int32, (1, 128), 1)
     low_a = lane < 64
     low_b = (lane % 64) < 32
-    rows = (hi - lo) * PITCH
-    here = LEAD + lo * PITCH
-    start = here - PITCH
-    more = rows + 2 * PITCH
-    first = first_buf[here : here + rows, :]
+    one = span_of(groups)
+    rows = (hi - lo) * one
+    first = rows_at(first_buf, lo - 1, hi + 1, 0, groups)
     shifted = jnp.where(
-        low_a, first_buf[start + 1 : start + 1 + more, :], first_buf[start - 1 : start - 1 + more, :]
+        low_a,
+        rows_at(first_buf, lo - 1, hi + 1, 1, groups),
+        rows_at(first_buf, lo - 1, hi + 1, -1, groups),
     )
-    across = jnp.where(
-        low_b, first_buf[here + PITCH : here + PITCH + rows, :], first_buf[start : start + rows, :]
-    )
-    both = jnp.where(low_b, shifted[2 * PITCH :], shifted[:rows])
+    across = jnp.where(low_b, first[2 * one :], first[:rows])
+    both = jnp.where(low_b, shifted[2 * one :], shifted[:rows])
     stacked = jnp.concatenate(
-        [first, across, shifted[PITCH : PITCH + rows], both], axis=1
+        [first[one : one + rows], across, shifted[one : one + rows], both], axis=1
     ).astype(jnp.bfloat16)
     made = jnp.dot(stacked, w2_full[...], preferred_element_type=jnp.float32)
     best = jnp.maximum(made[:, 0:128], made[:, 128:256])
     best = jnp.maximum(best, pltpu.roll(best, 64, 1))
     second = jnp.maximum(best + b2_full[...], 0.0)
-    second = jnp.where(inside_map(lo, hi, where) > 0.5, second, 0.0)
-    second_buf[here : here + rows, :] = second.astype(jnp.bfloat16).astype(jnp.float32)
-
-
-def conv3(lo, hi, w3_full, b3_ref, w4_ref, second_buf):
+    second = second * inside_map(lo, hi, groups, where)
+    put_rows(second_buf, lo, hi, groups, second.astype(jnp.bfloat16).astype(jnp.float32))
+
+
+def conv3(lo, hi, groups, w3_full, b3_ref, w4_ref, second_buf):
     lane = lax.broadcasted_iota(jnp.int32, (1, 128), 1)
     low_a = lane < 64
-    rows = (hi - lo) * PITCH
 
     def moved(k):
-        di, dj = k // 3, k % 3
-        begin = LEAD + (lo + dj - 1) * PITCH + di - 1
-        return second_buf[begin : begin + rows, :]
-
-    groups = []
+        return rows_at(second_buf, lo + k % 3 - 1, hi + k % 3 - 1, k // 3 - 1, groups)
+
+    taps = []
     for k in range(0, 9, 2):
-        groups.append(jnp.where(low_a, moved(k), moved(k + 1)) if k < 8 else moved(k))
-    stacked = jnp.concatenate(groups, axis=1).astype(jnp.bfloat16)
+        taps.append(jnp.where(low_a, moved(k), moved(k + 1)) if k < 8 else moved(k))
+    stacked = jnp.concatenate(taps, axis=1).astype(jnp.bfloat16)
     made = jnp.dot(stacked, w3_full[...], preferred_element_type=jnp.float32)
     third = jnp.maximum(made + b3_ref[...], 0.0).astype(jnp.bfloat16).astype(jnp.float32)
     weighted = third * w4_ref[...].astype(jnp.float32)
-    return jnp.sum(weighted.reshape(hi - lo, PITCH, 128), axis=2)
+    return jnp.sum(weighted.reshape(hi - lo, span_of(groups), 128), axis=2)
 
 
 def body(
@@ -624,7 +692,7 @@
     )
     kept = [
         (pltpu.SMEM if k < 4 else pltpu.VMEM)(operand.shape, operand.dtype)
-        for k, operand in enumerate(operands[:11])
+        for k, operand in enumerate(operands[:11]) if k not in (2, 3)
     ]
     scores, totals = pl.pallas_call(
         functools.partial(whole_kernel, chips, others, scale, cuts),
@@ -632,7 +700,7 @@
             pltpu.VMEM((tiles, tiles), f32),
             pltpu.SMEM((videos,), f32),
         ),
-        in_specs=[hbm] * len(operands),
+        in_specs=[hbm] * 2 + [smem] * 2 + [hbm] * (len(operands) - 4),
         out_specs=(vmem, smem),
         scratch_shapes=kept + [
             pltpu.VMEM(query_mat.shape, bf16),
@@ -653,9 +721,10 @@
             pltpu.VMEM((1, 128), f32),
             pltpu.VMEM((1, 128), f32),
             pltpu.VMEM((3 * frames, 384), bf16),
+            pltpu.VMEM((3 * frames, 384), bf16),
             pltpu.VMEM((-(-side // 8) * 8, 128), f32),
             pltpu.VMEM((senders * others, videos, 128), f32),
-            dma((11,)),
+            dma((9,)),
             dma(()),
             dma(()),
             dma(()),

time: 68.4 us -> 67.9 us (level)
  no operation moved by 1% of the time
where the time goes in v6:
time: 67.9 us; the launch traced here: 67.7 us
  Pallas kernels  64.5 us (95%)
  between operations  2.1 us (3%)
  local copies, waits for them, and re-layouts  1.12 us (2%)
    pallas_call x1, Pallas kernels, body(): pl.pallas_call(functools.partial(whole_kernel, chips, others, scale, cuts...  64.5 us

profile of v6, /device:TPU:0, one launch (start us, length us, event | category | flops | bytes accessed | tf_op | source)
XLA Modules:
  0.0 67.7 jit_solution(14878400662337733596)
XLA Ops:
  1.9 64.5 %whole.1 = (f32[32,32]{1,0:T(8,128)S(1)}, f32[2]{0:T(128)S(4)}) custom-call(s32[4,4]{1,0:T(4,128)} %pair_hbm.1, s32[2]{0:T(128)} %lengths_hbm.1, s32[1]{0:T(128)S(6)} %copy.19.len_ref, f32[1]{0:T(128)S(6)} %copy.20.b4_ref, f32[3,3,32]{2,1,0:T(4,128)} %w1_hbm.1, f32[1,32]{1,0:T(1,128)} %bitcast.20, bf16[9,32,64]{2,1,0:T(8,128)(2,1)} %bitcast.19, ...), custom_call_target="tpu_custom_call" | custom-call | tf_op jit(solution)/shard_map/whole/pallas_call | solution.py:697
  66.4 0.6 copy.17
  67.0 0.5 copy.18

commit v7 on v6

--- a/solution.py
+++ b/solution.py
@@ -67,9 +67,10 @@
     scores_ref, totals_ref,
     pair_ref, lengths_ref, w1_ref, b1_ref, w2_ref, b2_ref, w3_ref, b3_ref, w4_ref,
     q_buf, r_own, r_far, acc, sims_buf, map_buf, z_buf, x_buf, first_buf, second_buf,
-    w1_rep, w1_flat, w1_full, w2_full, w3_full, b1_full, b2_full, pick_full, pick_edge, score_buf, peaks_buf,
+    w1_rep, w1_flat, w1_full, w2_full, w3_full, b1_full, b2_full, pick_full, pick_edge,
+    score_buf, peaks_buf, edge_out, edge_in,
     small_sem, q_sem, own_sem, send_o, recv_o, send_x, recv_x, send_s, recv_s, send_h, recv_h,
-    send_p, recv_p, far_sem,
+    send_p, recv_p, far_sem, send_e, recv_e,
 ):
     regions, shard, depth = r_hbm.shape
     frames = q_hbm.shape[0] // regions
@@ -300,7 +301,41 @@
 
     moves = [(q, 0, g) for g in range(chunks) for q in (-1, 1)]
     moves += [(q, r, 0 if r < 0 else chunks - 1) for r in (-1, 1) for q in (-1, 1, 0)]
+    moves = [(q, r, g) for q, r, g in moves if r or g == last]
     moves = list(enumerate(moves))
+
+    def edge_copy(k, q):
+        side = (1 - q) // 2
+        return pltpu.make_async_remote_copy(
+            src_ref=edge_out.at[k, 1 - side],
+            dst_ref=edge_in.at[k, side],
+            send_sem=send_e.at[k, side],
+            recv_sem=recv_e.at[k, side],
+            device_id={"qry": me + q},
+            device_id_type=MESH,
+        )
+
+    def send_edges(k):
+        turned = jnp.transpose(map_buf[1, HALO : HALO + frames, :])
+        edge_out[k, 0] = turned[:HALO]
+        edge_out[k, 1] = turned[frames - HALO :]
+        for q in (-1, 1):
+
+            @pl.when(reachable(q, 0))
+            def _():
+                edge_copy(k, q).start()
+
+    def take_edges(k, stage):
+        for q in (-1, 1):
+
+            @pl.when(reachable(-q, 0))
+            def _():
+                edge_copy(k, q).wait_recv()
+                turned = jnp.transpose(edge_in[k, (1 - q) // 2])
+                lanes = slice(frames - HALO, frames) if q == 1 else slice(0, HALO)
+                for g in stage:
+                    rows = slice(HALO + g * width, HALO + (g + 1) * width)
+                    map_buf[1 - q, rows, lanes] = turned[g * width : (g + 1) * width]
 
     def spread(g):
         for b in range(senders):
@@ -342,6 +377,8 @@
 
     def network(k):
         halos(stages[k])
+        if stages[k]:
+            take_edges(k - 2 + min(chunks - 1, 2), stages[k])
         convolve(k, (0, 1, 2), pick_full, ALL, ALL)
 
     for k, g in enumerate(order[:-1]):
@@ -354,6 +391,8 @@
                 else:
                     keep(step, g, acc[...] + settle(step, g, lo, hi))
         spread(g)
+        if k >= chunks - 3:
+            send_edges(k - max(chunks - 3, 0))
         enqueue(limits[k], limits[k + 1])
     network(0)
 
@@ -424,6 +463,13 @@
         @pl.when(reachable(q, r))
         def _():
             halo_copy(k, q, r, g).wait_send()
+
+    for k in range(min(chunks - 1, 2)):
+        for q in (-1, 1):
+
+            @pl.when(reachable(q, 0))
+            def _():
+                edge_copy(k, q).wait_send()
 
     heard = all_of(
         peaks_buf.at[pl.ds(0, peers - 1)], {"qry": sibling}, send_p, recv_p
@@ -724,6 +770,8 @@
             pltpu.VMEM((3 * frames, 384), bf16),
             pltpu.VMEM((-(-side // 8) * 8, 128), f32),
             pltpu.VMEM((senders * others, videos, 128), f32),
+            pltpu.VMEM((2, 2, HALO, frames), f32),
+            pltpu.VMEM((2, 2, HALO, frames), f32),
             dma((9,)),
             dma(()),
             dma(()),
@@ -733,11 +781,13 @@
             dma((steps, chunks, pieces)),
             dma((steps,)),
             dma((steps, chunks, 3)),
-            dma((2 * chunks + 6,)),
-            dma((2 * chunks + 6,)),
+            dma((8,)),
+            dma((8,)),
             dma(()),
             dma(()),
             pltpu.SemaphoreType.REGULAR((max(1, others - 1),)),
+            dma((2, 2)),
+            dma((2, 2)),
         ],
         compiler_params=pltpu.CompilerParams(
             collective_id=0, has_side_effects=True, vmem_limit_bytes=56 << 20

time: 67.9 us -> 67.4 us (level)
  no operation moved by 1% of the time
where the time goes in v7:
time: 67.4 us; the launch traced here: 67.2 us
  Pallas kernels  64 us (95%)
  between operations  2.1 us (3%)
  local copies, waits for them, and re-layouts  1.12 us (2%)
    pallas_call x1, Pallas kernels, body(): pl.pallas_call(functools.partial(whole_kernel, chips, others, scale, cuts...  64 us

profile of v7, /device:TPU:0, one launch (start us, length us, event | category | flops | bytes accessed | tf_op | source)
XLA Modules:
  0.0 67.2 jit_solution(13601889458465677059)
XLA Ops:
  1.9 64.0 %whole.1 = (f32[32,32]{1,0:T(8,128)S(1)}, f32[2]{0:T(128)S(4)}) custom-call(s32[4,4]{1,0:T(4,128)} %pair_hbm.1, s32[2]{0:T(128)} %lengths_hbm.1, s32[1]{0:T(128)S(6)} %copy.19.len_ref, f32[1]{0:T(128)S(6)} %copy.20.b4_ref, f32[3,3,32]{2,1,0:T(4,128)} %w1_hbm.1, f32[1,32]{1,0:T(1,128)} %bitcast.20, bf16[9,32,64]{2,1,0:T(8,128)(2,1)} %bitcast.19, ...), custom_call_target="tpu_custom_call" | custom-call | tf_op jit(solution)/shard_map/whole/pallas_call | solution.py:743
  65.9 0.6 copy.17
  66.6 0.5 copy.18

commit v8 on v7

--- a/solution.py
+++ b/solution.py
@@ -109,7 +109,7 @@
         return pl.ds(pl.multiple_of(g * GROUP, GROUP), GROUP)
 
     def batches(g):
-        steps = (0, pieces - 3, pieces - 1, pieces) if g == last else (0, pieces - 2, pieces)
+        steps = (0, *range(pieces - 3, pieces + 1)) if g == last else (0, pieces - 2, pieces)
         return list(zip(steps[:-1], steps[1:]))
 
     def batch(g, p):
@@ -403,9 +403,10 @@
         arrive(step, last, pieces - 3)
         if step == 0:
             network(1)
+        acc[...] += settle(step, last, pieces - 3, pieces - 2)
         arrive(step, last, pieces - 2)
         arrive(step, last, pieces - 1)
-        acc[...] += settle(step, last, pieces - 3, pieces - 1)
+        acc[...] += settle(step, last, pieces - 2, pieces - 1)
         keep(step, last, acc[...] + settle(step, last, pieces - 1, pieces))
     spread(last)
     convolve(2, (1,), pick_full, ALL, INNER)
@@ -706,7 +707,7 @@
     chunks = shard // GROUP
     chips = senders // 2
     steps = max(1, chips - 1)
-    cuts = [depth * k // 6 // 128 * 128 for k in range(7)]
+    cuts = [depth * k // 30 // 128 * 128 for k in (0, 5, 10, 16, 22, 27, 30)]
     pieces = len(cuts) - 1
     tiles = frames // 4
     side = tiles + 4
@@ -780,7 +781,7 @@
             dma((steps,)),
             dma((steps, chunks, pieces)),
             dma((steps,)),
-            dma((steps, chunks, 3)),
+            dma((steps, chunks, 4)),
             dma((8,)),
             dma((8,)),
             dma(()),

time: 67.4 us -> 67.4 us (level)
  no operation moved by 1% of the time
where the time goes in v8:
time: 67.4 us; the launch traced here: 67.2 us
  Pallas kernels  64 us (95%)
  between operations  2.1 us (3%)
  local copies, waits for them, and re-layouts  1.12 us (2%)
    pallas_call x1, Pallas kernels, body(): pl.pallas_call(functools.partial(whole_kernel, chips, others, scale, cuts...  64 us

profile of v8, /device:TPU:0, one launch (start us, length us, event | category | flops | bytes accessed | tf_op | source)
XLA Modules:
  0.0 67.2 jit_solution(1122730010360979879)
XLA Ops:
  1.9 64.0 %whole.1 = (f32[32,32]{1,0:T(8,128)S(1)}, f32[2]{0:T(128)S(4)}) custom-call(s32[4,4]{1,0:T(4,128)} %pair_hbm.1, s32[2]{0:T(128)} %lengths_hbm.1, s32[1]{0:T(128)S(6)} %copy.19.len_ref, f32[1]{0:T(128)S(6)} %copy.20.b4_ref, f32[3,3,32]{2,1,0:T(4,128)} %w1_hbm.1, f32[1,32]{1,0:T(1,128)} %bitcast.20, bf16[9,32,64]{2,1,0:T(8,128)(2,1)} %bitcast.19, ...), custom_call_target="tpu_custom_call" | custom-call | tf_op jit(solution)/shard_map/whole/pallas_call | solution.py:744
  65.9 0.6 copy.17
  66.5 0.5 copy.18
